TPU v7x, 512 devices: a whole 4x4x16 slice. The times are simulated.
512 devices in a mesh: gx: 32 (over z, y_lo), gy: 16 (over y_hi, x, core).
Axes of the slice: x: 4, y: 4 (y_hi: 2, y_lo: 2; y = y_hi * 2 + y_lo), z: 16, core: 2. Of those that a mesh axis runs over, the one named last changes fastest.
Arguments:
- fields: float32 [5, 4, 1024, 2048], P(None, None, 'gx', 'gy'), may hold values from -6 to 6
- viscosity: float32 [4, 1024, 2048], P(None, 'gx', 'gy'), may hold values from 0.03 to 0.3
- precursor: float32 [5, 4, 512], P(None, None, 'gy'), may hold values from -6 to 6
- tile_index: int32 [2048], P('gy'), may hold values from 0 to 511, as said below
- fine_fields: float32 [8192, 5, 4, 4, 256], P(('gx', 'gy')), may hold values from -6 to 6
- fine_viscosity: float32 [8192, 4, 4, 256], P(('gx', 'gy')), may hold values from 0.03 to 0.3
- partner_gx: int32 [8192], P(('gx', 'gy')), may hold values from 0 to 31, as said below
- partner_col: int32 [8192], P(('gx', 'gy')), may hold values from 0 to 31
Outputs:
- fields_out: float32 [5, 4, 1024, 2048], P(None, None, 'gx', 'gy')
- fine_out: float32 [8192, 5, 4, 4, 256], P(('gx', 'gy'))
Inputs may be any that keep to these rules, and one draw needn't show every extreme that they name: `tile_index`: inlet cell y takes precursor cell (y + s) mod 512, where s is drawn for each aligned block of 128 cells. `partner_gx`: each device's tiles are glued to outer devices of its own gy row: exactly 2 tiles to each of 8 distinct gx indices; in every gy row one gx index receives 2 tiles from every device of the row.
All inputs are finite; a program needn't handle non-finite values.
Results may differ from a plain program's by a relative error of at most 0.00005.
Values sent between devices are 32-bit elements; how exact they have to be, the bound alone decides.
No kernel may reach another device: no remote copies, remote signals or barrier semaphores. Data moves between devices by JAX's collectives and lax.ppermute only.
A program may use at most 64 MiB of HBM per device.

v0:
```python
import jax
import jax.numpy as jnp
from jax import lax
from jax.sharding import PartitionSpec as P

CAP = 2


time_step = 0.2
vertical_mix = 0.1
coarse_penalty = 0.5
fine_penalty = 1.0


def padded_2(cells, sides, width):
    for axis, dim in sides:
        count = lax.axis_size(axis)
        head = lax.slice_in_dim(cells, 0, width, axis=dim)
        tail = lax.slice_in_dim(cells, cells.shape[dim] - width, cells.shape[dim], axis=dim)
        cells = jnp.concatenate(
            [
                lax.ppermute(tail, axis, [(i, (i + 1) % count) for i in range(count)]),
                cells,
                lax.ppermute(head, axis, [((i + 1) % count, i) for i in range(count)]),
            ],
            axis=dim,
        )
    return cells


def tendency(padded, spacing):
    nfield = padded.shape[-4] - 1
    state_part = padded[..., :nfield, :, :, :]
    visc_part = padded[..., nfield:, :, :, :]
    centre = state_part[..., 1:-1, 1:-1]
    q_east = state_part[..., 2:, 1:-1]
    q_west = state_part[..., :-2, 1:-1]
    q_north = state_part[..., 1:-1, 2:]
    q_south = state_part[..., 1:-1, :-2]
    u_flow = centre[..., 0:1, :, :, :]
    v_flow = centre[..., 1:2, :, :, :]
    nu_mid = visc_part[..., 1:-1, 1:-1]
    nu_east = 0.5 * (nu_mid + visc_part[..., 2:, 1:-1])
    nu_west = 0.5 * (nu_mid + visc_part[..., :-2, 1:-1])
    nu_north = 0.5 * (nu_mid + visc_part[..., 1:-1, 2:])
    nu_south = 0.5 * (nu_mid + visc_part[..., 1:-1, :-2])
    advect = (u_flow * (q_east - q_west) + v_flow * (q_north - q_south)) / (2.0 * spacing)
    diffuse = (
        nu_east * (q_east - centre)
        - nu_west * (centre - q_west)
        + nu_north * (q_north - centre)
        - nu_south * (centre - q_south)
    ) / (spacing * spacing)
    q_above = jnp.concatenate([centre[..., 1:, :, :], centre[..., -1:, :, :]], axis=-3)
    q_below = jnp.concatenate([centre[..., :1, :, :], centre[..., :-1, :, :]], axis=-3)
    return diffuse - advect + vertical_mix * (q_above - 2.0 * centre + q_below)


def coarsen_table(fine_width):
    fine_pos = jnp.arange(fine_width, dtype=jnp.int32)[:, None]
    coarse_pos = jnp.arange(fine_width // 2, dtype=jnp.int32)[None, :]
    weights = (
        0.5 * (fine_pos == 2 * coarse_pos)
        + 0.25 * (fine_pos == 2 * coarse_pos + 1)
        + 0.25 * (fine_pos == 2 * coarse_pos - 1)
        + 0.25 * ((coarse_pos == 0) & (fine_pos == 0))
    )
    return weights.astype(jnp.float32)


def refine_table(coarse_width):
    coarse_pos = jnp.arange(coarse_width, dtype=jnp.int32)[:, None]
    fine_pos = jnp.arange(2 * coarse_width, dtype=jnp.int32)[None, :]
    half_pos = fine_pos // 2
    upper_pos = jnp.minimum(half_pos + 1, coarse_width - 1)
    is_even = fine_pos % 2 == 0
    weights = jnp.where(
        is_even,
        1.0 * (coarse_pos == half_pos),
        0.5 * (coarse_pos == half_pos) + 0.5 * (coarse_pos == upper_pos),
    )
    return weights.astype(jnp.float32)


def on_device(
    fields, viscosity, precursor, tile_index, fine_fields, fine_viscosity, partner_gx, partner_col
):
    highest = lax.Precision.HIGHEST
    nfield, levels, columns, span_cells = fields.shape
    plane_total = precursor.shape[2] * lax.axis_size("gy")
    choose = (tile_index[:, None] == jnp.arange(plane_total, dtype=jnp.int32)[None, :]).astype(
        jnp.float32
    )
    inflow = jnp.einsum(
        "fzp,yp->fzy",
        lax.all_gather(precursor, "gy", axis=2, tiled=True),
        choose,
        precision=highest,
    )
    stacked = jnp.concatenate([fields, viscosity[None]], axis=0)
    padded = padded_2(stacked, (("gx", 2), ("gy", 3)), 1)
    at_inlet = lax.axis_index("gx") == 0
    at_outlet = lax.axis_index("gx") == lax.axis_size("gx") - 1
    inlet_ghost = jnp.concatenate([inflow, viscosity[None, :, 0, :]], axis=0)
    padded = padded.at[:, :, 0, 1:-1].set(jnp.where(at_inlet, inlet_ghost, padded[:, :, 0, 1:-1]))
    padded = padded.at[:, :, -1, 1:-1].set(
        jnp.where(at_outlet, stacked[:, :, -1, :], padded[:, :, -1, 1:-1])
    )
    coarse_rate = tendency(padded, 1.0)
    fine_stack = jnp.concatenate([fine_fields, fine_viscosity[:, None]], axis=1)
    fine_rate = tendency(
        jnp.pad(fine_stack, ((0, 0), (0, 0), (0, 0), (1, 1), (1, 1)), mode="edge"), 0.5
    )
    groups = lax.axis_size("gx")
    slot_count = groups * CAP
    target_hot = (partner_gx[:, None] == jnp.arange(groups, dtype=jnp.int32)[None, :]).astype(
        jnp.int32
    )
    before = jnp.cumsum(target_hot, axis=0) - target_hot
    rank_within = jnp.sum(before * target_hot, axis=1)
    slot_index = partner_gx * CAP + rank_within
    packing = (slot_index[:, None] == jnp.arange(slot_count, dtype=jnp.int32)[None, :]).astype(
        jnp.float32
    )
    col_hot = (partner_col[:, None] == jnp.arange(columns, dtype=jnp.int32)[None, :]).astype(
        jnp.float32
    )
    fine_trace = fine_fields[:, :, :, 0, :]
    to_coarse = coarsen_table(fine_trace.shape[-1])
    to_fine = refine_table(span_cells)
    sending = jnp.einsum("ts,tfzk->sfzk", packing, fine_trace, precision=highest)
    sending = sending.reshape((groups, CAP) + fine_trace.shape[1:])
    columns_out = jnp.einsum("ts,tc->sc", packing, col_hot, precision=highest).reshape(
        groups, CAP, columns
    )
    trace_in = lax.all_to_all(sending, "gx", split_axis=0, concat_axis=0, tiled=True)
    column_in = lax.all_to_all(columns_out, "gx", split_axis=0, concat_axis=0, tiled=True)
    coarse_in = jnp.einsum("gsfzw,wk->gsfzk", trace_in, to_coarse, precision=highest)
    matched = jnp.einsum("gsx,fzxy->gsfzy", column_in, fields, precision=highest)
    answer = jnp.einsum("gsfzk,kw->gsfzw", matched, to_fine, precision=highest)
    returned = lax.all_to_all(answer, "gx", split_axis=0, concat_axis=0, tiled=True)
    mismatch, column_in, returned = (coarse_in - matched, column_in, returned)
    coarse_sat = coarse_penalty * jnp.einsum(
        "gsx,gsfzy->fzxy", column_in, mismatch, precision=highest
    )
    fields_out = fields + time_step * (coarse_rate + coarse_sat)
    coming_back = jnp.einsum(
        "ts,sfzw->tfzw",
        packing,
        returned.reshape((slot_count,) + returned.shape[2:]),
        precision=highest,
    )
    fine_sat = fine_penalty * (coming_back - fine_trace)
    total_rate = fine_rate.at[:, :, :, 0, :].add(fine_sat)
    fine_out = fine_fields + time_step * total_rate
    return (fields_out, fine_out)


def solution(mesh):
    return jax.shard_map(
        on_device,
        mesh=mesh,
        in_specs=(
            P(None, None, "gx", "gy"),
            P(None, "gx", "gy"),
            P(None, None, "gy"),
            P("gy"),
            P(("gx", "gy"), None, None, None, None),
            P(("gx", "gy"), None, None, None),
            P(("gx", "gy")),
            P(("gx", "gy")),
        ),
        out_specs=(P(None, None, "gx", "gy"), P(("gx", "gy"), None, None, None, None)),
        check_vma=False,
    )
```

profile of v0, /device:TPU:58, one launch (start us, length us, event | category | flops | bytes accessed | tf_op | source)
XLA Modules:
  0.0 180.7 jit_solution(5967769567230981480)
XLA Ops:
  0.6 0.7 fusion.91
  1.4 0.8 select_reduce_fusion
  2.2 0.7 multiply_add_fusion.2
  2.9 1.6 fusion.89
  4.5 16.3 %all-to-all-start.1 = ((f32[32,2,32]{2,1,0:T(2,128)}), f32[32,2,32]{2,1,0:T(2,128)S(1)}, u32[]{:S(2)}, u32[]{:S(2)}) async-start(f32[32,2,32]{2,1,0:T(2,128)} %bitcast.19), calls=%async_computation.1 | async-start | bytes 65536 | tf_op jit(solution)/shard_map/all_to_all | solution.py:137
  20.7 2.1 %copy.142 = f32[16,5,4,4,256]{4,0,2,1,3:T(8,128)S(1)} copy(f32[16,5,4,4,256]{4,3,2,1,0:T(4,128)} %param.18) | data formatting | bytes 2621440 | tf_op args[4]
  22.8 0.8 fusion.31
  23.6 1.9 %copy.143 = f32[32,2,5,4,256]{4,3,2,1,0:T(4,128)} copy(f32[32,2,5,4,256]{4,0,3,2,1:T(8,128)S(1)} %fusion.31) | data formatting | bytes 2621440 | tf_op jit(solution)/shard_map/ts,tfzk->sfzk/dot_general | solution.py:131
  25.5 6.8 %all-to-all-done.1 = f32[32,2,32]{2,1,0:T(2,128)S(1)} async-done(((f32[32,2,32]{2,1,0:T(2,128)}), f32[32,2,32]{2,1,0:T(2,128)S(1)}, u32[]{:S(2)}, u32[]{:S(2)}) %all-to-all-start.1) | async-done | bytes 8224 | tf_op jit(solution)/shard_map/all_to_all | solution.py:137
  32.3 6.5 %all-to-all-start = ((f32[32,2,5,4,256]{4,3,2,1,0:T(4,128)}), f32[32,2,5,4,256]{4,3,2,1,0:T(4,128)}, u32[]{:S(2)}, u32[]{:S(2)}) async-start(f32[32,2,5,4,256]{4,3,2,1,0:T(4,128)} %copy.143), calls=%async_computation | async-start | bytes 2621440 | tf_op jit(solution)/shard_map/all_to_all | solution.py:136
  38.8 3.4 %collective-permute-start = (f32[6,4,1,128]{3,2,1,0:T(1,128)S(1)}, f32[6,4,1,128]{3,2,1,0:T(1,128)S(1)}, u32[]{:S(2)}, u32[]{:S(2)}) collective-permute-start(f32[6,4,1,128]{3,2,1,0:T(1,128)S(1)} %get-tuple-element.74), channel_id=1, source_target_pairs={{0,16},{16,32},{32,48},{48,64},{64,80},{80,96},{96,112},{112,128},... | collective-permute-start | bytes 36872 | tf_op jit(solution)/shard_map/ppermute | solution.py:22
  42.2 2.5 %collective-permute-start.1 = (f32[6,4,1,128]{3,2,1,0:T(1,128)S(1)}, f32[6,4,1,128]{3,2,1,0:T(1,128)S(1)}, u32[]{:S(2)}, u32[]{:S(2)}) collective-permute-start(f32[6,4,1,128]{3,2,1,0:T(1,128)S(1)} %get-tuple-element.75), channel_id=1, source_target_pairs={{16,0},{32,16},{48,32},{64,48},{80,64},{96,80},{112,96},{128,112},... | collective-permute-start | bytes 36872 | tf_op jit(solution)/shard_map/ppermute | solution.py:24
  44.9 1.1 slice_bitcast_fusion.1
  46.0 0.2 copy.156
  46.4 24.0 %all_gather.3 = f32[5,4,512]{0,1,2:T(4,128)} all-gather(f32[5,4,32]{0,1,2:T(4,128)S(1)} %copy.138), channel_id=1, replica_groups=mesh['gx'=32,'gy'=16] {'gy'}, dimensions={2}, use_global_device_ids=true | all-gather | bytes 43520 | tf_op jit(solution)/shard_map/all_gather | solution.py:96
  70.4 1.6 copy.167
  72.0 0.6 fusion.110
  72.7 0.7 fusion.29
  73.4 1.2 fusion.49
  74.6 1.9 %copy.163 = f32[32,2,5,4,256]{4,3,2,1,0:T(4,128)} copy(f32[32,2,5,4,256]{4,0,3,2,1:T(8,128)S(1)} %fusion.49) | data formatting | bytes 2621440 | tf_op jit(solution)/shard_map/gsfzk,kw->gsfzw/dot_general | solution.py:140
  76.5 27.4 %all-to-all-done = f32[32,2,5,4,256]{4,3,2,1,0:T(4,128)} async-done(((f32[32,2,5,4,256]{4,3,2,1,0:T(4,128)}), f32[32,2,5,4,256]{4,3,2,1,0:T(4,128)}, u32[]{:S(2)}, u32[]{:S(2)}) %all-to-all-start) | async-done | bytes 1310752 | tf_op jit(solution)/shard_map/all_to_all | solution.py:136
  103.9 4.6 %all-to-all-start.2 = ((f32[32,2,5,4,256]{4,3,2,1,0:T(4,128)}), f32[32,2,5,4,256]{4,3,2,1,0:T(4,128)}, u32[]{:S(2)}, u32[]{:S(2)}) async-start(f32[32,2,5,4,256]{4,3,2,1,0:T(4,128)} %copy.163), calls=%async_computation.2 | async-start | bytes 2621440 | tf_op jit(solution)/shard_map/all_to_all | solution.py:141
  108.6 0.2 pad_maximum_fusion
  108.9 0.4 copy-done.5
  109.3 0.3 fusion.43
  109.6 0.4 fusion.104
  110.1 0.2 fusion.37
  110.3 0.3 fusion.106
  110.6 3.0 %fusion.2 = f32[16,5,4,4,256]{4,0,2,1,3:T(8,128)} fusion(f32[16,5,1,4,256]{4,0,2,1,3:T(8,128)S(1)} %get-tuple-element.59, f32[16,5,3,4,256]{4,0,2,1,3:T(8,128)S(1)} %get-tuple-element.61, f32[16,5,3,4,256]{4,0,2,1,3:T(8,128)S(1)} %get-tuple-element.60, f32[16,5,1,4,256]{4,0,2,1,3:T(8,128)S(1)} %get-tuple-element.58, f32[16,5,4,4,256]{4,0,2,1,3:T(8,128)S(1)} %copy.142, ...), kind=kLoop, calls=%fused_computation.16 | loop fusion | flops 12124160 | bytes 7882752 | tf_op jit(solution)/shard_map/add | solution.py:56
  113.7 0.2 fusion.109
  113.9 0.3 copy.134
  114.1 1.9 %collective-permute-start.2 = (f32[6,4,34,1]{2,1,3,0:T(4,128)S(1)}, f32[6,4,34,1]{2,1,3,0:T(4,128)S(1)}, u32[]{:S(2)}, u32[]{:S(2)}) collective-permute-start(f32[6,4,34,1]{2,1,3,0:T(4,128)S(1)} %copy.134), channel_id=1, source_target_pairs={{0,1},{1,2},{2,3},{3,4},{4,5},{5,6},{6,7},{7,8},{8,9},{9,10},{10,1... | collective-permute-start | bytes 9800 | tf_op jit(solution)/shard_map/ppermute | solution.py:22
  116.0 0.3 copy.135
  116.3 3.8 %collective-permute-start.3 = (f32[6,4,34,1]{2,1,3,0:T(4,128)S(1)}, f32[6,4,34,1]{2,1,3,0:T(4,128)S(1)}, u32[]{:S(2)}, u32[]{:S(2)}) collective-permute-start(f32[6,4,34,1]{2,1,3,0:T(4,128)S(1)} %copy.135), channel_id=1, source_target_pairs={{1,0},{2,1},{3,2},{4,3},{5,4},{6,5},{7,6},{8,7},{9,8},{10,9},{11,1... | collective-permute-start | bytes 9800 | tf_op jit(solution)/shard_map/ppermute | solution.py:24
  120.2 1.1 copy.136
  121.3 1.1 copy.137
  122.4 1.7 pad_maximum_fusion.13
  124.1 5.1 %scatter.6 = f32[6,4,34,130]{3,2,1,0:T(8,128)S(1)} dynamic-update-slice(f32[6,4,34,130]{3,2,1,0:T(8,128)S(1)} %pad_maximum_fusion.13, f32[6,4,1,128]{3,2,1,0:T(1,128)S(1)} %broadcast_select_fusion.1, s32[]{:T(128)} %constant.156.clone.1, s32[]{:T(128)} %constant.156.clone.1, s32[]{:T(128)} %bitcast.5, s32[]{:T(128)} %bitcast.6) | dynamic-update-slice | bytes 24580 | tf_op jit(solution)/shard_map/scatter | solution.py:105
  129.3 3.8 %scatter.9 = f32[6,4,34,130]{3,2,1,0:T(8,128)S(1)} dynamic-update-slice(f32[6,4,34,130]{3,2,1,0:T(8,128)S(1)} %scatter.6, f32[6,4,1,128]{3,2,1,0:T(1,128)S(1)} %broadcast_select_fusion, s32[]{:T(128)} %constant.156.clone.1, s32[]{:T(128)} %constant.156.clone.1, s32[]{:T(128)} %constant.158.clone.1, s32[]{:T(128)} %constant.159.clone.1) | dynamic-update-slice | bytes 24580 | tf_op jit(solution)/shard_map/scatter | solution.py:106
  133.2 0.2 fusion.71
  133.4 0.2 fusion.108
  133.6 2.8 %fusion.7 = f32[32,2,5,4,128]{4,0,3,2,1:T(8,128)S(1)} fusion(f32[32,2,5,4,128]{4,0,3,2,1:T(8,128)S(1)} %fusion.29, f32[32,2,5,4,256]{4,3,2,1,0:T(4,128)} %all-to-all-done, s32[128]{0:T(128)S(1)} %get-tuple-element.79, s32[128]{0:T(128)S(1)} %broadcast_add_fusion.1, s32[128]{0:T(128)S(1)} %get-tuple-element.78, pred[128]{0:T(512)(128)(4,1)S(1)} %iota_compare_fusion.16, ...), kind=kOutput, calls=%fused_computation.22 | convolution fusion | flops 503840768 | bytes 2623360 | tf_op jit(solution)/shard_map/gsfzw,wk->gsfzk/dot_general | solution.py:138
  136.4 0.5 convolution_bitcast_fusion
  136.9 1.2 fusion.28
  138.1 35.8 %all-to-all-done.2 = f32[32,2,5,4,256]{4,3,2,1,0:T(4,128)} async-done(((f32[32,2,5,4,256]{4,3,2,1,0:T(4,128)}), f32[32,2,5,4,256]{4,3,2,1,0:T(4,128)}, u32[]{:S(2)}, u32[]{:S(2)}) %all-to-all-start.2) | async-done | bytes 1310752 | tf_op jit(solution)/shard_map/all_to_all | solution.py:141
  173.9 2.7 %fusion.19 = f32[16,5,4,4,256]{4,0,2,1,3:T(8,128)} fusion(f32[16,5,4,4,256]{4,0,2,1,3:T(8,128)} %fusion.2, f32[64,5,4,256]{3,2,1,0:T(4,128)} %bitcast.36, f32[16,5,4,4,256]{4,0,2,1,3:T(8,128)S(1)} %copy.142, s32[16]{0:T(128)S(1)} %multiply_add_fusion.2), kind=kOutput, calls=%fused_computation.27 | convolution fusion | flops 63079424 | bytes 2293824 | tf_op jit(solution)/shard_map/ts,sfzw->tfzw/dot_general | solution.py:147
  176.6 2.2 %multiply_add_fusion = f32[16,5,4,4,256]{4,0,2,1,3:T(8,128)S(1)} fusion(f32[16,5,4,4,256]{4,0,2,1,3:T(8,128)} %fusion.19, f32[16,5,4,4,256]{4,3,2,1,0:T(4,128)S(1)} %copy-done.1), kind=kLoop, calls=%fused_computation.21 | loop fusion | flops 655360 | bytes 3932160 | tf_op jit(solution)/shard_map/add | solution.py:155
  178.8 1.9 %copy.166 = f32[16,5,4,4,256]{4,3,2,1,0:T(4,128)} copy(f32[16,5,4,4,256]{4,0,2,1,3:T(8,128)S(1)} %multiply_add_fusion) | data formatting | bytes 2621440
  (36 shorter events, 1.1 us)
Async XLA Ops:
  4.5 27.9 %all-to-all-start.1 = ((f32[32,2,32]{2,1,0:T(2,128)}), f32[32,2,32]{2,1,0:T(2,128)S(1)}, u32[]{:S(2)}, u32[]{:S(2)}) async-start(f32[32,2,32]{2,1,0:T(2,128)} %bitcast.19), calls=%async_computation.1 | async-start | bytes 65536 | tf_op jit(solution)/shard_map/all_to_all | solution.py:137
  25.5 13.3 %copy-start = (f32[5,4,32,128]{3,2,1,0:T(8,128)S(1)}, f32[5,4,32,128]{3,2,1,0:T(8,128)}, u32[]{:S(2)}) copy-start(f32[5,4,32,128]{3,2,1,0:T(8,128)} %param.14) | copy-start | bytes 983044
  25.5 13.3 %copy-start.2 = (f32[4,32,128]{2,1,0:T(8,128)S(1)}, f32[4,32,128]{2,1,0:T(8,128)}, u32[]{:S(2)}) copy-start(f32[4,32,128]{2,1,0:T(8,128)} %param.15) | copy-start | bytes 196612
  25.5 19.2 %copy-start.3 = (f32[16,4,4,256]{3,2,1,0:T(4,128)S(1)}, f32[16,4,4,256]{3,2,1,0:T(4,128)}, u32[]{:S(2)}) copy-start(f32[16,4,4,256]{3,2,1,0:T(4,128)} %param.19) | copy-start | bytes 786436
  32.3 71.6 %all-to-all-start = ((f32[32,2,5,4,256]{4,3,2,1,0:T(4,128)}), f32[32,2,5,4,256]{4,3,2,1,0:T(4,128)}, u32[]{:S(2)}, u32[]{:S(2)}) async-start(f32[32,2,5,4,256]{4,3,2,1,0:T(4,128)} %copy.143), calls=%async_computation | async-start | bytes 2621440 | tf_op jit(solution)/shard_map/all_to_all | solution.py:136
  38.8 74.8 %collective-permute-start = (f32[6,4,1,128]{3,2,1,0:T(1,128)S(1)}, f32[6,4,1,128]{3,2,1,0:T(1,128)S(1)}, u32[]{:S(2)}, u32[]{:S(2)}) collective-permute-start(f32[6,4,1,128]{3,2,1,0:T(1,128)S(1)} %get-tuple-element.74), channel_id=1, source_target_pairs={{0,16},{16,32},{32,48},{48,64},{64,80},{80,96},{96,112},{112,128},... | collective-permute-start | bytes 36872 | tf_op jit(solution)/shard_map/ppermute | solution.py:22
  42.2 4.1 %copy-start.4 = (f32[5,4,32]{2,1,0:T(4,128)S(1)}, f32[5,4,32]{2,1,0:T(4,128)}, u32[]{:S(2)}) copy-start(f32[5,4,32]{2,1,0:T(4,128)} %param.16) | copy-start | bytes 7684
  42.2 71.4 %collective-permute-start.1 = (f32[6,4,1,128]{3,2,1,0:T(1,128)S(1)}, f32[6,4,1,128]{3,2,1,0:T(1,128)S(1)}, u32[]{:S(2)}, u32[]{:S(2)}) collective-permute-start(f32[6,4,1,128]{3,2,1,0:T(1,128)S(1)} %get-tuple-element.75), channel_id=1, source_target_pairs={{16,0},{32,16},{48,32},{64,48},{80,64},{96,80},{112,96},{128,112},... | collective-permute-start | bytes 36872 | tf_op jit(solution)/shard_map/ppermute | solution.py:24
  103.9 70.0 %all-to-all-start.2 = ((f32[32,2,5,4,256]{4,3,2,1,0:T(4,128)}), f32[32,2,5,4,256]{4,3,2,1,0:T(4,128)}, u32[]{:S(2)}, u32[]{:S(2)}) async-start(f32[32,2,5,4,256]{4,3,2,1,0:T(4,128)} %copy.163), calls=%async_computation.2 | async-start | bytes 2621440 | tf_op jit(solution)/shard_map/all_to_all | solution.py:141
  108.6 0.7 copy-start.5
  114.1 6.0 %collective-permute-start.2 = (f32[6,4,34,1]{2,1,3,0:T(4,128)S(1)}, f32[6,4,34,1]{2,1,3,0:T(4,128)S(1)}, u32[]{:S(2)}, u32[]{:S(2)}) collective-permute-start(f32[6,4,34,1]{2,1,3,0:T(4,128)S(1)} %copy.134), channel_id=1, source_target_pairs={{0,1},{1,2},{2,3},{3,4},{4,5},{5,6},{6,7},{7,8},{8,9},{9,10},{10,1... | collective-permute-start | bytes 9800 | tf_op jit(solution)/shard_map/ppermute | solution.py:22
  116.3 5.0 %collective-permute-start.3 = (f32[6,4,34,1]{2,1,3,0:T(4,128)S(1)}, f32[6,4,34,1]{2,1,3,0:T(4,128)S(1)}, u32[]{:S(2)}, u32[]{:S(2)}) collective-permute-start(f32[6,4,34,1]{2,1,3,0:T(4,128)S(1)} %copy.135), channel_id=1, source_target_pairs={{1,0},{2,1},{3,2},{4,3},{5,4},{6,5},{7,6},{8,7},{9,8},{10,9},{11,1... | collective-permute-start | bytes 9800 | tf_op jit(solution)/shard_map/ppermute | solution.py:24
  138.1 38.5 %copy-start.1 = (f32[16,5,4,4,256]{4,3,2,1,0:T(4,128)S(1)}, f32[16,5,4,4,256]{4,3,2,1,0:T(4,128)}, u32[]{:S(2)}) copy-start(f32[16,5,4,4,256]{4,3,2,1,0:T(4,128)} %param.18) | copy-start | bytes 3932164
where the time goes:
time: 181 us
  waiting for transfers between devices  70.1 us (39%)
  starting transfers between devices  38.9 us (21%)
  local copies, waits for them, and re-layouts  24.8 us (14%)
  blocking collectives  24 us (13%)
  other arithmetic  11.4 us (6%)
  matrix products  10.6 us (6%)
    all_to_all x1, waiting for transfers between devices, on_device(): lax.all_to_all(answer, 'gx', split_axis=0, concat_axis=0, tiled=True)  35.8 us
    all_to_all x1, waiting for transfers between devices, on_device(): lax.all_to_all(sending, 'gx', split_axis=0, concat_axis=0, tiled=True)  27.4 us
    all_gather x1, blocking collectives, on_device(): lax.all_gather(precursor, 'gy', axis=2, tiled=True)  24 us
    all_to_all x1, starting transfers between devices, on_device(): lax.all_to_all(columns_out, 'gx', split_axis=0, concat_axis=0, tiled=True)  16.3 us
    all_to_all x1, waiting for transfers between devices, on_device(): lax.all_to_all(columns_out, 'gx', split_axis=0, concat_axis=0, tiled=True)  6.83 us
    all_to_all x1, starting transfers between devices, on_device(): lax.all_to_all(sending, 'gx', split_axis=0, concat_axis=0, tiled=True)  6.45 us
    ppermute x2, starting transfers between devices, padded_2(): lax.ppermute(head, axis, [((i + 1) % count, i) for i in range(count)])  6.29 us
    ppermute x2, starting transfers between devices, padded_2(): lax.ppermute(tail, axis, [(i, (i + 1) % count) for i in range(count)])  5.29 us
  transfers between devices with their start and end apart: 7, of which 4 were waited for; matrix products, arithmetic and copies ran while one was open for 20% of the time, Pallas kernels for 0%

commit v1 on v0

v1 whole, which is shorter than its diff:
```python
import jax
import jax.numpy as jnp
from jax import lax
from jax.experimental import pallas as pl
from jax.experimental.pallas import tpu as pltpu
from jax.sharding import PartitionSpec as P


CAP = 2
VMEM_BYTES = 16 * 2**20
HIGHEST = lax.Precision.HIGHEST


time_step = 0.2
vertical_mix = 0.1
coarse_penalty = 0.5
fine_penalty = 1.0

WHOLE = pl.BlockSpec(memory_space=pltpu.VMEM)
SCALARS = pl.BlockSpec(memory_space=pltpu.SMEM)


def cost(flops, *arrays):
    return pl.CostEstimate(
        flops=flops, transcendentals=0, bytes_accessed=sum(4 * a.size for a in arrays)
    )


def coarsen_weights(width):
    fine = lax.broadcasted_iota(jnp.int32, (width, width // 2), 0)
    middle = 2 * lax.broadcasted_iota(jnp.int32, (width, width // 2), 1)
    sides = (fine == middle + 1) | (fine == middle - 1)
    weights = jnp.where(fine == middle, 0.5, jnp.where(sides, 0.25, 0.0))
    return weights + jnp.where((fine == 0) & (middle == 0), 0.25, 0.0)


def refine_weights(count):
    coarse = lax.broadcasted_iota(jnp.int32, (count, 2 * count), 0)
    fine = lax.broadcasted_iota(jnp.int32, (count, 2 * count), 1)
    lower = fine // 2
    upper = jnp.minimum((fine + 1) // 2, count - 1)
    return jnp.where(coarse == lower, 0.5, 0.0) + jnp.where(coarse == upper, 0.5, 0.0)


def ring_shift(cells, axis, step):
    count = lax.axis_size(axis)
    return lax.ppermute(cells, axis, [(i, (i + step) % count) for i in range(count)])


def pack_kernel(gx_ref, fine_ref, out_ref, slot_ref, seen_ref):
    groups = seen_ref.shape[0]
    tiles, nfield, levels, _, width = fine_ref.shape

    def clear(group, carry):
        seen_ref[group] = 0
        return carry

    lax.fori_loop(0, groups, clear, 0)
    out_ref[...] = jnp.zeros_like(out_ref)
    trace = fine_ref[:, :, :, 0, :].reshape(tiles * nfield * levels, width)
    cells = jnp.dot(
        trace, coarsen_weights(width), precision=HIGHEST, preferred_element_type=jnp.float32
    ).reshape(tiles, nfield, levels, width // 2)
    for i in range(tiles):
        target = gx_ref[i]
        slot = target * CAP + seen_ref[target]
        seen_ref[target] = seen_ref[target] + 1
        slot_ref[i] = slot
        out_ref[slot] = cells[i]


def pack_traces(partner_gx, fine_fields, groups):
    tiles, nfield, levels, _, width = fine_fields.shape
    sent = jax.ShapeDtypeStruct((groups * CAP, nfield, levels, width // 2), jnp.float32)
    return pl.pallas_call(
        pack_kernel,
        out_shape=(sent, jax.ShapeDtypeStruct((tiles,), jnp.int32)),
        in_specs=[SCALARS, WHOLE],
        out_specs=(WHOLE, SCALARS),
        scratch_shapes=[pltpu.SMEM((groups,), jnp.int32)],
        cost_estimate=cost(10**8, fine_fields, sent),
        compiler_params=pltpu.CompilerParams(vmem_limit_bytes=VMEM_BYTES),
        name="pack_traces",
    )(partner_gx, fine_fields)


def finish_kernel(slot_ref, back_ref, part_ref, out_ref, stage_ref, sems):
    step = pl.program_id(0)
    tiles, nfield, levels, _, width = part_ref.shape
    total = stage_ref.shape[0]

    def fetch(tile):
        return pltpu.make_async_copy(
            back_ref.at[slot_ref[tile]], stage_ref.at[tile], sems.at[tile]
        )

    @pl.when(step == 0)
    def _():
        for tile in range(total):
            fetch(tile).start()

    for i in range(tiles):
        fetch(step * tiles + i).wait()
    cells = stage_ref[pl.ds(step * tiles, tiles)].reshape(tiles * nfield * levels, width // 2)
    fine = jnp.dot(
        cells, refine_weights(width // 2), precision=HIGHEST, preferred_element_type=jnp.float32
    ).reshape(tiles, nfield, levels, width)
    out_ref[...] = part_ref[...]
    out_ref[:, :, :, 0, :] = part_ref[:, :, :, 0, :] + (time_step * fine_penalty) * fine


def finish_tiles(slots, back, part, block=4):
    tiles, nfield, levels, rows, width = part.shape
    spec = pl.BlockSpec((block, nfield, levels, rows, width), lambda i: (i, 0, 0, 0, 0))
    return pl.pallas_call(
        finish_kernel,
        grid=(tiles // block,),
        out_shape=jax.ShapeDtypeStruct(part.shape, jnp.float32),
        in_specs=[SCALARS, pl.BlockSpec(memory_space=pl.ANY), spec],
        out_specs=spec,
        scratch_shapes=[
            pltpu.VMEM((tiles, nfield, levels, width // 2), jnp.float32),
            pltpu.SemaphoreType.DMA((tiles,)),
        ],
        cost_estimate=cost(10**8, part, part, back),
        compiler_params=pltpu.CompilerParams(vmem_limit_bytes=VMEM_BYTES),
        name="finish_tiles",
    )(slots, back, part)


def neighbour(cells, axis, step):
    count = cells.shape[axis]
    if step > 0:
        parts = [(1, count), (count - 1, count)]
    else:
        parts = [(0, 1), (0, count - 1)]
    return jnp.concatenate([lax.slice_in_dim(cells, *p, axis=axis) for p in parts], axis=axis)


def fine_kernel(q_ref, nu_ref, out_ref):
    def one_tile(tile, carry):
        nu = nu_ref[tile]
        nu_east = 2.0 * (nu + neighbour(nu, 1, 1))
        nu_west = 2.0 * (nu + neighbour(nu, 1, -1))
        nu_north = 2.0 * (nu + neighbour(nu, 2, 1))
        nu_south = 2.0 * (nu + neighbour(nu, 2, -1))
        u_flow = q_ref[tile, 0]
        v_flow = q_ref[tile, 1]
        glued = lax.broadcasted_iota(jnp.int32, nu.shape, 1) == 0
        for field in range(q_ref.shape[1]):
            q = q_ref[tile, field]
            east, west = neighbour(q, 1, 1), neighbour(q, 1, -1)
            north, south = neighbour(q, 2, 1), neighbour(q, 2, -1)
            above, below = neighbour(q, 0, 1), neighbour(q, 0, -1)
            diffuse = (
                nu_east * (east - q)
                - nu_west * (q - west)
                + nu_north * (north - q)
                - nu_south * (q - south)
            )
            advect = u_flow * (east - west) + v_flow * (north - south)
            rate = diffuse - advect + vertical_mix * (above - 2.0 * q + below)
            out_ref[tile, field] = q + time_step * (
                rate - jnp.where(glued, fine_penalty * q, 0.0)
            )
        return carry

    lax.fori_loop(0, q_ref.shape[0], one_tile, 0)


def fine_step(fine_fields, fine_viscosity, block=4):
    tiles, nfield, levels, rows, width = fine_fields.shape
    spec = pl.BlockSpec((block, nfield, levels, rows, width), lambda i: (i, 0, 0, 0, 0))
    return pl.pallas_call(
        fine_kernel,
        grid=(tiles // block,),
        out_shape=jax.ShapeDtypeStruct(fine_fields.shape, jnp.float32),
        in_specs=[spec, pl.BlockSpec((block, levels, rows, width), lambda i: (i, 0, 0, 0))],
        out_specs=spec,
        cost_estimate=cost(10**8, fine_fields, fine_fields, fine_viscosity),
        compiler_params=pltpu.CompilerParams(vmem_limit_bytes=VMEM_BYTES),
        name="fine_step",
    )(fine_fields, fine_viscosity)


def coarse_kernel(
    wanted_ref,
    q_ref,
    nu_ref,
    west_ref,
    east_ref,
    south_ref,
    north_ref,
    came_ref,
    sent_ref,
    out_ref,
    sat_ref,
):
    nfield, levels, columns, span = q_ref.shape
    lane = lax.broadcasted_iota(jnp.int32, (columns, span), 1)
    sat_ref[...] = jnp.zeros_like(sat_ref)

    def add_slot(slot, carry):
        column = wanted_ref[slot]

        @pl.when(column >= 0)
        def _():
            sat_ref[column] += came_ref[slot] - sent_ref[slot]

        return carry

    lax.fori_loop(0, came_ref.shape[0], add_slot, 0)

    def around(q, which, level):
        row = which * levels + level
        east = jnp.concatenate([q[1:], east_ref[row : row + 1, :]], axis=0)
        west = jnp.concatenate([west_ref[row : row + 1, :], q[:-1]], axis=0)
        north = jnp.where(
            lane == span - 1, north_ref[:, row : row + 1], pltpu.roll(q, span - 1, 1)
        )
        south = jnp.where(lane == 0, south_ref[:, row : row + 1], pltpu.roll(q, 1, 1))
        return east, west, north, south

    for level in range(levels):
        nu = nu_ref[level]
        nu_east, nu_west, nu_north, nu_south = (
            0.5 * (nu + other) for other in around(nu, nfield, level)
        )
        u_flow = q_ref[0, level]
        v_flow = q_ref[1, level]
        for field in range(nfield):
            q = q_ref[field, level]
            east, west, north, south = around(q, field, level)
            above = q_ref[field, min(level + 1, levels - 1)]
            below = q_ref[field, max(level - 1, 0)]
            diffuse = (
                nu_east * (east - q)
                - nu_west * (q - west)
                + nu_north * (north - q)
                - nu_south * (q - south)
            )
            advect = 0.5 * (u_flow * (east - west) + v_flow * (north - south))
            rate = diffuse - advect + vertical_mix * (above - 2.0 * q + below)
            sat = coarse_penalty * sat_ref[:, field, level, :]
            out_ref[field, level] = q + time_step * (rate + sat)


def coarse_step(wanted, fields, viscosity, west, east, south, north, came, sent):
    nfield, levels, columns, span = fields.shape
    return pl.pallas_call(
        coarse_kernel,
        out_shape=jax.ShapeDtypeStruct(fields.shape, jnp.float32),
        in_specs=[SCALARS] + [WHOLE] * 8,
        out_specs=WHOLE,
        scratch_shapes=[pltpu.VMEM((columns, nfield, levels, span), jnp.float32)],
        cost_estimate=cost(10**8, fields, fields, came),
        compiler_params=pltpu.CompilerParams(vmem_limit_bytes=VMEM_BYTES),
        name="coarse_step",
    )(wanted, fields, viscosity, west, east, south, north, came, sent)


def on_device(
    fields, viscosity, precursor, tile_index, fine_fields, fine_viscosity, partner_gx, partner_col
):
    nfield, levels, columns, span_cells = fields.shape
    tiles = partner_gx.shape[0]
    groups = lax.axis_size("gx")
    my_gx = lax.axis_index("gx")
    my_gy = lax.axis_index("gy")
    block = (groups, CAP, nfield, levels, span_cells)

    sending, slots = pack_traces(partner_gx, fine_fields, groups)
    trace_in = lax.all_to_all(sending.reshape(block), "gx", split_axis=0, concat_axis=0, tiled=True)

    rows = jnp.concatenate([fields, viscosity[None]], axis=0)
    halo = (nfield + 1) * levels
    request = jnp.concatenate([partner_gx, partner_col]).astype(jnp.float32)[None, :]
    request = jnp.pad(request, ((0, 0), (0, span_cells - 2 * tiles)))
    low_row = rows[:, :, 0, :].reshape(halo, span_cells)
    high_row = rows[:, :, -1, :].reshape(halo, span_cells)
    from_west = ring_shift(jnp.concatenate([high_row, request], axis=0), "gx", 1)
    from_east = ring_shift(low_row, "gx", -1)
    asked = jnp.concatenate([request, from_west[halo:]], axis=0)
    while asked.shape[0] < groups:
        asked = jnp.concatenate([asked, ring_shift(asked, "gx", asked.shape[0])], axis=0)
    order = (
        jnp.arange(groups)[None, :] == (my_gx - jnp.arange(groups)[:, None]) % groups
    ).astype(jnp.float32)
    asked = jnp.einsum("sj,jc->sc", order, asked[:, : 2 * tiles], precision=HIGHEST)
    mine = asked[:, :tiles] == my_gx.astype(jnp.float32)
    earlier = jnp.arange(tiles)[None, :] < jnp.arange(tiles)[:, None]
    before = jnp.sum(jnp.where(earlier, mine[:, None, :], False).astype(jnp.int32), axis=2)
    wanted = []
    for rank in range(CAP):
        chosen = mine & (before == rank)
        wanted.append(jnp.sum(jnp.where(chosen, asked[:, tiles:] + 1.0, 0.0), axis=1) - 1.0)
    wanted = jnp.stack(wanted, axis=1)
    column_in = (wanted[:, :, None] == jnp.arange(columns, dtype=jnp.float32)).astype(jnp.float32)
    answer = jnp.einsum("gsx,fzxy->gsfzy", column_in, fields, precision=HIGHEST)
    returned = lax.all_to_all(answer, "gx", split_axis=0, concat_axis=0, tiled=True)

    low_col = rows[:, :, :, 0].reshape(halo, columns)
    high_col = rows[:, :, :, -1].reshape(halo, columns)
    width = precursor.shape[2]
    shard = precursor.reshape(nfield * levels, width)
    from_south = ring_shift(jnp.concatenate([high_col, shard], axis=0), "gy", 1)
    from_north = ring_shift(low_col, "gy", -1)
    shards = jnp.stack([shard, from_south[halo:]])
    count = lax.axis_size("gy")
    while shards.shape[0] < count:
        shards = jnp.concatenate([shards, ring_shift(shards, "gy", shards.shape[0])], axis=0)
    position = ((my_gy - tile_index // width) % count) * width + tile_index % width
    choose = (position[:, None] == jnp.arange(count * width)[None, :]).astype(jnp.float32)
    inflow = jnp.einsum(
        "jro,yjo->ry", shards, choose.reshape(-1, count, width), precision=HIGHEST
    )

    inlet = jnp.concatenate([inflow, viscosity[:, 0, :]], axis=0)
    west = jnp.where(my_gx == 0, inlet, from_west[:halo])
    east = jnp.where(my_gx == groups - 1, high_row, from_east)
    slab = (groups * CAP,) + block[2:]
    fields_out = coarse_step(
        wanted.reshape(groups * CAP).astype(jnp.int32),
        fields,
        viscosity,
        west,
        east,
        from_south[:halo].T,
        from_north.T,
        trace_in.reshape(slab),
        answer.reshape(slab),
    )

    part = fine_step(fine_fields, fine_viscosity)
    fine_out = finish_tiles(slots, returned.reshape(slab), part)
    return (fields_out, fine_out)


def solution(mesh):
    return jax.shard_map(
        on_device,
        mesh=mesh,
        in_specs=(
            P(None, None, "gx", "gy"),
            P(None, "gx", "gy"),
            P(None, None, "gy"),
            P("gy"),
            P(("gx", "gy"), None, None, None, None),
            P(("gx", "gy"), None, None, None),
            P(("gx", "gy")),
            P(("gx", "gy")),
        ),
        out_specs=(P(None, None, "gx", "gy"), P(("gx", "gy"), None, None, None, None)),
        check_vma=False,
    )
```

time: 181 us -> 159 us (0.88)
  the two profiles are of different devices: /device:TPU:58 before, /device:TPU:16 now
where the time goes in v1:
time: 159 us; the launch traced here: 158 us
  starting transfers between devices  70.5 us (44%)
  waiting for transfers between devices  64.3 us (40%)
  Pallas kernels  12.6 us (8%)
  local copies, waits for them, and re-layouts  7.15 us (4%)
  matrix products  2.06 us (1%)
    ppermute x11, waiting for transfers between devices, ring_shift(): lax.ppermute(cells, axis, [(i, (i + step) % count) for i in range(count)])  64.3 us
    ppermute x11, starting transfers between devices, ring_shift(): lax.ppermute(cells, axis, [(i, (i + step) % count) for i in range(count)])  42.5 us
    all_to_all x1, starting transfers between devices, on_device(): lax.all_to_all(sending.reshape(block), 'gx', split_axis=0, concat_axis=0,...  16.2 us
    all_to_all x1, starting transfers between devices, on_device(): lax.all_to_all(answer, 'gx', split_axis=0, concat_axis=0, tiled=True)  11.7 us
    unnamed x28, local copies, waits for them, and re-layouts  4.56 us
    pallas_call x1, Pallas kernels, finish_tiles(): pl.pallas_call(finish_kernel, grid=(tiles // block,), out_shape=jax.Shape...  3.74 us
    pallas_call x1, Pallas kernels, coarse_step(): pl.pallas_call(coarse_kernel, out_shape=jax.ShapeDtypeStruct(fields.shape...  3.56 us
  transfers between devices with their start and end apart: 13, of which 9 were waited for; matrix products, arithmetic and copies ran while one was open for 5% of the time, Pallas kernels for 4%

profile of v1, /device:TPU:16, one launch (start us, length us, event | category | flops | bytes accessed | tf_op | source)
XLA Modules:
  0.0 158.4 jit_solution(151879505979967620)
XLA Ops:
  0.6 1.3 copy-done
  2.0 0.7 copy-done.7
  2.6 2.2 %pack_traces.1 = (f32[64,5,4,128]{3,2,1,0:T(4,128)}, s32[16]{0:T(128)S(1)}) custom-call(s32[16]{0:T(128)S(1)} %copy-done.7, f32[16,5,4,4,256]{4,3,2,1,0:T(4,128)S(1)} %copy-done), custom_call_target="tpu_custom_call" | custom-call | flops 100000000 | bytes 1966080 | tf_op jit(solution)/shard_map/pack_traces/pallas_call | solution.py:75
  4.8 16.2 %all-to-all-start = ((f32[32,2,5,4,128]{4,3,2,1,0:T(4,128)}), f32[32,2,5,4,128]{4,3,2,1,0:T(4,128)S(1)}, u32[]{:S(2)}, u32[]{:S(2)}) async-start(f32[32,2,5,4,128]{4,3,2,1,0:T(4,128)} %bitcast.12), calls=%async_computation | async-start | bytes 1310720 | tf_op jit(solution)/shard_map/all_to_all | solution.py:273
  21.0 0.1 add_convert_fusion
  21.2 3.7 %collective-permute-start = (f32[25,128]{1,0:T(8,128)S(1)}, f32[25,128]{1,0:T(8,128)S(1)}, u32[]{:S(2)}, u32[]{:S(2)}) collective-permute-start(f32[25,128]{1,0:T(8,128)S(1)} %pad_maximum_fusion.4), channel_id=1, source_target_pairs={{0,16},{16,32},{32,48},{48,64},{64,80},{80,96},{96,112},{112,128},... | collective-permute-start | bytes 38408 | tf_op jit(solution)/shard_map/ppermute | solution.py:47
  24.9 27.0 %collective-permute-done = f32[25,128]{1,0:T(8,128)S(1)} collective-permute-done((f32[25,128]{1,0:T(8,128)S(1)}, f32[25,128]{1,0:T(8,128)S(1)}, u32[]{:S(2)}, u32[]{:S(2)}) %collective-permute-start) | collective-permute-done | bytes 12832 | tf_op jit(solution)/shard_map/ppermute | solution.py:47
  51.9 1.9 %collective-permute-start.1 = (f32[2,128]{1,0:T(2,128)S(1)}, f32[2,128]{1,0:T(2,128)S(1)}, u32[]{:S(2)}, u32[]{:S(2)}) collective-permute-start(f32[2,128]{1,0:T(2,128)S(1)} %pad_maximum_fusion.9), channel_id=1, source_target_pairs={{0,32},{16,48},{32,64},{48,80},{64,96},{80,112},{96,128},{112,144}... | collective-permute-start | bytes 3080 | tf_op jit(solution)/shard_map/ppermute | solution.py:47
  53.8 4.8 %collective-permute-done.1 = f32[2,128]{1,0:T(2,128)S(1)} collective-permute-done((f32[2,128]{1,0:T(2,128)S(1)}, f32[2,128]{1,0:T(2,128)S(1)}, u32[]{:S(2)}, u32[]{:S(2)}) %collective-permute-start.1) | collective-permute-done | bytes 1056 | tf_op jit(solution)/shard_map/ppermute | solution.py:47
  58.6 1.9 %collective-permute-start.2 = (f32[4,128]{1,0:T(4,128)S(1)}, f32[4,128]{1,0:T(4,128)S(1)}, u32[]{:S(2)}, u32[]{:S(2)}) collective-permute-start(f32[4,128]{1,0:T(4,128)S(1)} %pad_maximum_fusion.8), channel_id=1, source_target_pairs={{0,64},{16,80},{32,96},{48,112},{64,128},{80,144},{96,160},{112,17... | collective-permute-start | bytes 6152 | tf_op jit(solution)/shard_map/ppermute | solution.py:47
  60.5 5.7 %collective-permute-done.2 = f32[4,128]{1,0:T(4,128)S(1)} collective-permute-done((f32[4,128]{1,0:T(4,128)S(1)}, f32[4,128]{1,0:T(4,128)S(1)}, u32[]{:S(2)}, u32[]{:S(2)}) %collective-permute-start.2) | collective-permute-done | bytes 2080 | tf_op jit(solution)/shard_map/ppermute | solution.py:47
  66.2 6.7 %collective-permute-start.3 = (f32[8,128]{1,0:T(8,128)S(1)}, f32[8,128]{1,0:T(8,128)S(1)}, u32[]{:S(2)}, u32[]{:S(2)}) collective-permute-start(f32[8,128]{1,0:T(8,128)S(1)} %pad_maximum_fusion.7), channel_id=1, source_target_pairs={{0,128},{16,144},{32,160},{48,176},{64,192},{80,208},{96,224},{112... | collective-permute-start | bytes 12296 | tf_op jit(solution)/shard_map/ppermute | solution.py:47
  72.9 2.7 %collective-permute-done.3 = f32[8,128]{1,0:T(8,128)S(1)} collective-permute-done((f32[8,128]{1,0:T(8,128)S(1)}, f32[8,128]{1,0:T(8,128)S(1)}, u32[]{:S(2)}, u32[]{:S(2)}) %collective-permute-start.3) | collective-permute-done | bytes 4128 | tf_op jit(solution)/shard_map/ppermute | solution.py:47
  75.6 11.7 %collective-permute-start.4 = (f32[16,128]{1,0:T(8,128)S(1)}, f32[16,128]{1,0:T(8,128)S(1)}, u32[]{:S(2)}, u32[]{:S(2)}) collective-permute-start(f32[16,128]{1,0:T(8,128)S(1)} %concatenate.65), channel_id=1, source_target_pairs={{0,256},{16,272},{32,288},{48,304},{64,320},{80,336},{96,352},{112... | collective-permute-start | bytes 24584 | tf_op jit(solution)/shard_map/ppermute | solution.py:47
  87.3 2.5 %collective-permute-done.4 = f32[16,128]{1,0:T(8,128)S(1)} collective-permute-done((f32[16,128]{1,0:T(8,128)S(1)}, f32[16,128]{1,0:T(8,128)S(1)}, u32[]{:S(2)}, u32[]{:S(2)}) %collective-permute-start.4) | collective-permute-done | bytes 8224 | tf_op jit(solution)/shard_map/ppermute | solution.py:47
  89.9 0.2 fusion.10
  90.1 0.1 convert_reduce_fusion
  90.3 0.5 fusion.3
  90.8 1.3 copy.56
  92.1 11.7 %all-to-all-start.1 = ((f32[32,2,5,4,128]{4,3,2,1,0:T(4,128)}), f32[32,2,5,4,128]{4,3,2,1,0:T(4,128)}, u32[]{:S(2)}, u32[]{:S(2)}) async-start(f32[32,2,5,4,128]{4,3,2,1,0:T(4,128)} %copy.56), calls=%async_computation.1 | async-start | bytes 1310720 | tf_op jit(solution)/shard_map/all_to_all | solution.py:300
  103.8 5.8 %collective-permute-start.9 = (f32[24,128]{1,0:T(8,128)S(1)}, f32[24,128]{1,0:T(8,128)S(1)}, u32[]{:S(2)}, u32[]{:S(2)}) collective-permute-start(f32[24,128]{1,0:T(8,128)S(1)} %bitcast.45), channel_id=1, source_target_pairs={{0,496},{16,0},{32,16},{48,32},{64,48},{80,64},{96,80},{112,96},{1... | collective-permute-start | bytes 36872 | tf_op jit(solution)/shard_map/ppermute | solution.py:47
  109.6 0.4 fusion.2
  110.0 0.1 copy.55
  110.1 1.9 %collective-permute-start.10 = (f32[24,32]{0,1:T(8,128)S(1)}, f32[24,32]{0,1:T(8,128)S(1)}, u32[]{:S(2)}, u32[]{:S(2)}) collective-permute-start(f32[24,32]{0,1:T(8,128)S(1)} %copy.55), channel_id=1, source_target_pairs={{0,15},{1,0},{2,1},{3,2},{4,3},{5,4},{6,5},{7,6},{8,7},{9,8},{10,9... | collective-permute-start | bytes 9224 | tf_op jit(solution)/shard_map/ppermute | solution.py:47
  112.1 0.1 copy.48
  112.1 0.1 copy.47
  112.2 0.1 pad_maximum_fusion.5
  112.3 2.4 %collective-permute-start.5 = (f32[44,32]{0,1:T(8,128)S(1)}, f32[44,32]{0,1:T(8,128)S(1)}, u32[]{:S(2)}, u32[]{:S(2)}) collective-permute-start(f32[44,32]{0,1:T(8,128)S(1)} %pad_maximum_fusion.5), channel_id=1, source_target_pairs={{0,1},{1,2},{2,3},{3,4},{4,5},{5,6},{6,7},{7,8},{8,9},{9,10},{10,1... | collective-permute-start | bytes 16904 | tf_op jit(solution)/shard_map/ppermute | solution.py:47
  114.7 0.1 copy.52
  114.8 0.6 constant_dynamic-update-slice_fusion.4
  115.5 3.1 %fine_step.1.part_ref = f32[16,5,4,4,256]{4,3,2,1,0:T(4,128)S(1)} custom-call(f32[16,5,4,4,256]{4,3,2,1,0:T(4,128)S(1)} %copy-done.1, f32[16,4,4,256]{3,2,1,0:T(4,128)S(1)} %copy-done.6), custom_call_target="tpu_custom_call" | custom-call | flops 100000000 | bytes 2883584 | tf_op jit(solution)/shard_map/fine_step/pallas_call | solution.py:174
  118.6 2.4 %collective-permute-done.5 = f32[44,32]{0,1:T(8,128)S(1)} collective-permute-done((f32[44,32]{0,1:T(8,128)S(1)}, f32[44,32]{0,1:T(8,128)S(1)}, u32[]{:S(2)}, u32[]{:S(2)}) %collective-permute-start.5) | collective-permute-done | bytes 5664 | tf_op jit(solution)/shard_map/ppermute | solution.py:47
  121.0 0.1 slice_bitcast_fusion.1
  121.1 1.9 %collective-permute-start.6 = (f32[2,20,32]{1,2,0:T(8,128)S(1)}, f32[2,20,32]{1,2,0:T(8,128)S(1)}, u32[]{:S(2)}, u32[]{:S(2)}) collective-permute-start(f32[2,20,32]{1,2,0:T(8,128)S(1)} %pad_maximum_fusion.3), channel_id=1, source_target_pairs={{0,2},{1,3},{2,4},{3,5},{4,6},{5,7},{6,8},{7,9},{8,10},{9,11},{10,... | collective-permute-start | bytes 15368 | tf_op jit(solution)/shard_map/ppermute | solution.py:47
  123.0 0.7 constant_dynamic-update-slice_fusion.3
  123.7 6.9 %collective-permute-done.6 = f32[2,20,32]{1,2,0:T(8,128)S(1)} collective-permute-done((f32[2,20,32]{1,2,0:T(8,128)S(1)}, f32[2,20,32]{1,2,0:T(8,128)S(1)}, u32[]{:S(2)}, u32[]{:S(2)}) %collective-permute-start.6) | collective-permute-done | bytes 5152 | tf_op jit(solution)/shard_map/ppermute | solution.py:47
  130.5 1.9 %collective-permute-start.7 = (f32[4,20,32]{1,2,0:T(8,128)S(1)}, f32[4,20,32]{1,2,0:T(8,128)S(1)}, u32[]{:S(2)}, u32[]{:S(2)}) collective-permute-start(f32[4,20,32]{1,2,0:T(8,128)S(1)} %pad_maximum_fusion.2), channel_id=1, source_target_pairs={{0,4},{1,5},{2,6},{3,7},{4,8},{5,9},{6,10},{7,11},{8,12},{9,13},{1... | collective-permute-start | bytes 30728 | tf_op jit(solution)/shard_map/ppermute | solution.py:47
  132.5 0.6 constant_dynamic-update-slice_fusion.2
  133.1 7.5 %collective-permute-done.7 = f32[4,20,32]{1,2,0:T(8,128)S(1)} collective-permute-done((f32[4,20,32]{1,2,0:T(8,128)S(1)}, f32[4,20,32]{1,2,0:T(8,128)S(1)}, u32[]{:S(2)}, u32[]{:S(2)}) %collective-permute-start.7) | collective-permute-done | bytes 10272 | tf_op jit(solution)/shard_map/ppermute | solution.py:47
  140.6 2.7 %collective-permute-start.8 = (f32[8,20,32]{1,2,0:T(8,128)S(1)}, f32[8,20,32]{1,2,0:T(8,128)S(1)}, u32[]{:S(2)}, u32[]{:S(2)}) collective-permute-start(f32[8,20,32]{1,2,0:T(8,128)S(1)} %pad_maximum_fusion.1), channel_id=1, source_target_pairs={{0,8},{1,9},{2,10},{3,11},{4,12},{5,13},{6,14},{7,15},{8,0},{9,1},... | collective-permute-start | bytes 61448 | tf_op jit(solution)/shard_map/ppermute | solution.py:47
  143.3 0.6 constant_dynamic-update-slice_fusion.1
  143.9 0.1 copy.46
  144.0 0.1 convert_element_type.30.wanted_ref
  144.1 4.9 %collective-permute-done.8 = f32[8,20,32]{1,2,0:T(8,128)S(1)} collective-permute-done((f32[8,20,32]{1,2,0:T(8,128)S(1)}, f32[8,20,32]{1,2,0:T(8,128)S(1)}, u32[]{:S(2)}, u32[]{:S(2)}) %collective-permute-start.8) | collective-permute-done | bytes 20512 | tf_op jit(solution)/shard_map/ppermute | solution.py:47
  149.0 0.7 constant_dynamic-update-slice_fusion
  149.7 1.4 convolution_bitcast_fusion
  151.1 3.6 %coarse_step.1 = f32[5,4,32,128]{3,2,1,0:T(8,128)} custom-call(s32[64]{0:T(128)S(1)} %convert_element_type.30.wanted_ref, f32[5,4,32,128]{3,2,1,0:T(8,128)S(1)} %copy-done.2, f32[4,32,128]{2,1,0:T(8,128)S(1)} %copy-done.5, f32[24,128]{1,0:T(8,128)S(1)} %slice_select_fusion.west_ref, f32[24,128]{1,0:T(8,128)S(1)} %broadcast_select_fusion.east_ref, ...), custom_call_target="tpu_custom_call" | custom-call | flops 100000000 | bytes 1310720 | tf_op jit(solution)/shard_map/coarse_step/pallas_call | solution.py:250
  154.6 3.7 %finish_tiles.1 = f32[16,5,4,4,256]{4,3,2,1,0:T(4,128)} custom-call(s32[16]{0:T(128)S(1)} %get-tuple-element.5.slot_ref, f32[64,5,4,128]{3,2,1,0:T(4,128)} %bitcast.18.back_ref, f32[16,5,4,4,256]{4,3,2,1,0:T(4,128)S(1)} %fine_step.1.part_ref), custom_call_target="tpu_custom_call" | custom-call | flops 100000000 | bytes 3276800 | tf_op jit(solution)/shard_map/finish_tiles/pallas_call | solution.py:115
  (52 shorter events, 0.3 us)
Async XLA Ops:
  0.6 1.3 copy-start
  1.9 0.7 copy-start.7
  2.6 18.4 %copy-start.8 = (s32[16]{0:T(128)S(1)}, s32[16]{0:T(128)}, u32[]{:S(2)}) copy-start(s32[16]{0:T(128)} %gx_ref.1) | copy-start | bytes 196
  2.6 18.4 %copy-start.10 = (s32[16]{0:T(128)S(1)}, s32[16]{0:T(128)}, u32[]{:S(2)}) copy-start(s32[16]{0:T(128)} %param.15) | copy-start | bytes 196
  2.6 18.5 %copy-start.2 = (f32[5,4,32,128]{3,2,1,0:T(8,128)S(1)}, f32[5,4,32,128]{3,2,1,0:T(8,128)}, u32[]{:S(2)}) copy-start(f32[5,4,32,128]{3,2,1,0:T(8,128)} %q_ref.2) | copy-start | bytes 983044
  2.6 18.5 %copy-start.5 = (f32[4,32,128]{2,1,0:T(8,128)S(1)}, f32[4,32,128]{2,1,0:T(8,128)}, u32[]{:S(2)}) copy-start(f32[4,32,128]{2,1,0:T(8,128)} %nu_ref.2) | copy-start | bytes 196612
  4.8 87.2 %all-to-all-start = ((f32[32,2,5,4,128]{4,3,2,1,0:T(4,128)}), f32[32,2,5,4,128]{4,3,2,1,0:T(4,128)S(1)}, u32[]{:S(2)}, u32[]{:S(2)}) async-start(f32[32,2,5,4,128]{4,3,2,1,0:T(4,128)} %bitcast.12), calls=%async_computation | async-start | bytes 1310720 | tf_op jit(solution)/shard_map/all_to_all | solution.py:273
  21.2 30.7 %collective-permute-start = (f32[25,128]{1,0:T(8,128)S(1)}, f32[25,128]{1,0:T(8,128)S(1)}, u32[]{:S(2)}, u32[]{:S(2)}) collective-permute-start(f32[25,128]{1,0:T(8,128)S(1)} %pad_maximum_fusion.4), channel_id=1, source_target_pairs={{0,16},{16,32},{32,48},{48,64},{64,80},{80,96},{96,112},{112,128},... | collective-permute-start | bytes 38408 | tf_op jit(solution)/shard_map/ppermute | solution.py:47
  51.9 6.7 %collective-permute-start.1 = (f32[2,128]{1,0:T(2,128)S(1)}, f32[2,128]{1,0:T(2,128)S(1)}, u32[]{:S(2)}, u32[]{:S(2)}) collective-permute-start(f32[2,128]{1,0:T(2,128)S(1)} %pad_maximum_fusion.9), channel_id=1, source_target_pairs={{0,32},{16,48},{32,64},{48,80},{64,96},{80,112},{96,128},{112,144}... | collective-permute-start | bytes 3080 | tf_op jit(solution)/shard_map/ppermute | solution.py:47
  58.6 7.6 %collective-permute-start.2 = (f32[4,128]{1,0:T(4,128)S(1)}, f32[4,128]{1,0:T(4,128)S(1)}, u32[]{:S(2)}, u32[]{:S(2)}) collective-permute-start(f32[4,128]{1,0:T(4,128)S(1)} %pad_maximum_fusion.8), channel_id=1, source_target_pairs={{0,64},{16,80},{32,96},{48,112},{64,128},{80,144},{96,160},{112,17... | collective-permute-start | bytes 6152 | tf_op jit(solution)/shard_map/ppermute | solution.py:47
  66.2 9.4 %collective-permute-start.3 = (f32[8,128]{1,0:T(8,128)S(1)}, f32[8,128]{1,0:T(8,128)S(1)}, u32[]{:S(2)}, u32[]{:S(2)}) collective-permute-start(f32[8,128]{1,0:T(8,128)S(1)} %pad_maximum_fusion.7), channel_id=1, source_target_pairs={{0,128},{16,144},{32,160},{48,176},{64,192},{80,208},{96,224},{112... | collective-permute-start | bytes 12296 | tf_op jit(solution)/shard_map/ppermute | solution.py:47
  75.6 14.3 %collective-permute-start.4 = (f32[16,128]{1,0:T(8,128)S(1)}, f32[16,128]{1,0:T(8,128)S(1)}, u32[]{:S(2)}, u32[]{:S(2)}) collective-permute-start(f32[16,128]{1,0:T(8,128)S(1)} %concatenate.65), channel_id=1, source_target_pairs={{0,256},{16,272},{32,288},{48,304},{64,320},{80,336},{96,352},{112... | collective-permute-start | bytes 24584 | tf_op jit(solution)/shard_map/ppermute | solution.py:47
  90.7 21.3 %copy-start.9 = (f32[5,4,32]{2,1,0:T(4,128)S(1)}, f32[5,4,32]{2,1,0:T(4,128)}, u32[]{:S(2)}) copy-start(f32[5,4,32]{2,1,0:T(4,128)} %param.10) | copy-start | bytes 7684
  92.0 23.4 %copy-start.11 = (s32[128]{0:T(128)S(1)}, s32[128]{0:T(128)}, u32[]{:S(2)}) copy-start(s32[128]{0:T(128)} %param.11) | copy-start | bytes 1540
  92.0 23.4 %copy-start.1 = (f32[16,5,4,4,256]{4,3,2,1,0:T(4,128)S(1)}, f32[16,5,4,4,256]{4,3,2,1,0:T(4,128)}, u32[]{:S(2)}) copy-start(f32[16,5,4,4,256]{4,3,2,1,0:T(4,128)} %q_ref.3) | copy-start | bytes 3932164
  92.0 23.4 %copy-start.6 = (f32[16,4,4,256]{3,2,1,0:T(4,128)S(1)}, f32[16,4,4,256]{3,2,1,0:T(4,128)}, u32[]{:S(2)}) copy-start(f32[16,4,4,256]{3,2,1,0:T(4,128)} %nu_ref.3) | copy-start | bytes 786436
  92.0 23.4 %copy-start.3 = (f32[32,2,5,4,128]{4,3,2,1,0:T(4,128)}, f32[32,2,5,4,128]{4,3,2,1,0:T(4,128)S(1)}, u32[]{:S(2)}) copy-start(f32[32,2,5,4,128]{4,3,2,1,0:T(4,128)S(1)} %all-to-all-done) | copy-start | bytes 1966084
  92.1 62.6 %all-to-all-start.1 = ((f32[32,2,5,4,128]{4,3,2,1,0:T(4,128)}), f32[32,2,5,4,128]{4,3,2,1,0:T(4,128)}, u32[]{:S(2)}, u32[]{:S(2)}) async-start(f32[32,2,5,4,128]{4,3,2,1,0:T(4,128)} %copy.56), calls=%async_computation.1 | async-start | bytes 1310720 | tf_op jit(solution)/shard_map/all_to_all | solution.py:300
  103.8 29.3 %collective-permute-start.9 = (f32[24,128]{1,0:T(8,128)S(1)}, f32[24,128]{1,0:T(8,128)S(1)}, u32[]{:S(2)}, u32[]{:S(2)}) collective-permute-start(f32[24,128]{1,0:T(8,128)S(1)} %bitcast.45), channel_id=1, source_target_pairs={{0,496},{16,0},{32,16},{48,32},{64,48},{80,64},{96,80},{112,96},{1... | collective-permute-start | bytes 36872 | tf_op jit(solution)/shard_map/ppermute | solution.py:47
  110.1 41.0 %collective-permute-start.10 = (f32[24,32]{0,1:T(8,128)S(1)}, f32[24,32]{0,1:T(8,128)S(1)}, u32[]{:S(2)}, u32[]{:S(2)}) collective-permute-start(f32[24,32]{0,1:T(8,128)S(1)} %copy.55), channel_id=1, source_target_pairs={{0,15},{1,0},{2,1},{3,2},{4,3},{5,4},{6,5},{7,6},{8,7},{9,8},{10,9... | collective-permute-start | bytes 9224 | tf_op jit(solution)/shard_map/ppermute | solution.py:47
  112.3 8.7 %collective-permute-start.5 = (f32[44,32]{0,1:T(8,128)S(1)}, f32[44,32]{0,1:T(8,128)S(1)}, u32[]{:S(2)}, u32[]{:S(2)}) collective-permute-start(f32[44,32]{0,1:T(8,128)S(1)} %pad_maximum_fusion.5), channel_id=1, source_target_pairs={{0,1},{1,2},{2,3},{3,4},{4,5},{5,6},{6,7},{7,8},{8,9},{9,10},{10,1... | collective-permute-start | bytes 16904 | tf_op jit(solution)/shard_map/ppermute | solution.py:47
  118.6 32.5 %copy-start.4 = (f32[32,2,5,4,128]{4,3,2,1,0:T(4,128)S(1)}, f32[32,2,5,4,128]{4,3,2,1,0:T(4,128)}, u32[]{:S(2)}) copy-start(f32[32,2,5,4,128]{4,3,2,1,0:T(4,128)} %copy-done.3) | copy-start | bytes 1966084
  121.1 9.5 %collective-permute-start.6 = (f32[2,20,32]{1,2,0:T(8,128)S(1)}, f32[2,20,32]{1,2,0:T(8,128)S(1)}, u32[]{:S(2)}, u32[]{:S(2)}) collective-permute-start(f32[2,20,32]{1,2,0:T(8,128)S(1)} %pad_maximum_fusion.3), channel_id=1, source_target_pairs={{0,2},{1,3},{2,4},{3,5},{4,6},{5,7},{6,8},{7,9},{8,10},{9,11},{10,... | collective-permute-start | bytes 15368 | tf_op jit(solution)/shard_map/ppermute | solution.py:47
  130.5 10.1 %collective-permute-start.7 = (f32[4,20,32]{1,2,0:T(8,128)S(1)}, f32[4,20,32]{1,2,0:T(8,128)S(1)}, u32[]{:S(2)}, u32[]{:S(2)}) collective-permute-start(f32[4,20,32]{1,2,0:T(8,128)S(1)} %pad_maximum_fusion.2), channel_id=1, source_target_pairs={{0,4},{1,5},{2,6},{3,7},{4,8},{5,9},{6,10},{7,11},{8,12},{9,13},{1... | collective-permute-start | bytes 30728 | tf_op jit(solution)/shard_map/ppermute | solution.py:47
  140.6 8.4 %collective-permute-start.8 = (f32[8,20,32]{1,2,0:T(8,128)S(1)}, f32[8,20,32]{1,2,0:T(8,128)S(1)}, u32[]{:S(2)}, u32[]{:S(2)}) collective-permute-start(f32[8,20,32]{1,2,0:T(8,128)S(1)} %pad_maximum_fusion.1), channel_id=1, source_target_pairs={{0,8},{1,9},{2,10},{3,11},{4,12},{5,13},{6,14},{7,15},{8,0},{9,1},... | collective-permute-start | bytes 61448 | tf_op jit(solution)/shard_map/ppermute | solution.py:47

commit v2 on v1

--- a/solution.py
+++ b/solution.py
@@ -47,41 +47,96 @@
     return lax.ppermute(cells, axis, [(i, (i + step) % count) for i in range(count)])
 
 
-def pack_kernel(gx_ref, fine_ref, out_ref, slot_ref, seen_ref):
-    groups = seen_ref.shape[0]
-    tiles, nfield, levels, _, width = fine_ref.shape
+def pack_kernel(gx_ref, col_ref, fine_ref, out_ref, slot_ref, trace_ref, seen_ref, sems):
+    groups, rows = out_ref.shape[:2]
+    tiles, nfield, levels, width = trace_ref.shape
+    slab = (rows - 1) // CAP
+    chunk = tiles // sems.shape[0]
+
+    def fetch(part):
+        some = pl.ds(part * chunk, chunk)
+        return pltpu.make_async_copy(
+            fine_ref.at[some, :, :, 0, :], trace_ref.at[some], sems.at[part]
+        )
+
+    for part in range(tiles // chunk):
+        fetch(part).start()
 
     def clear(group, carry):
         seen_ref[group] = 0
         return carry
 
     lax.fori_loop(0, groups, clear, 0)
-    out_ref[...] = jnp.zeros_like(out_ref)
-    trace = fine_ref[:, :, :, 0, :].reshape(tiles * nfield * levels, width)
-    cells = jnp.dot(
-        trace, coarsen_weights(width), precision=HIGHEST, preferred_element_type=jnp.float32
-    ).reshape(tiles, nfield, levels, width // 2)
-    for i in range(tiles):
-        target = gx_ref[i]
-        slot = target * CAP + seen_ref[target]
-        seen_ref[target] = seen_ref[target] + 1
-        slot_ref[i] = slot
-        out_ref[slot] = cells[i]
-
-
-def pack_traces(partner_gx, fine_fields, groups):
+    out_ref[:, : rows - 1] = jnp.zeros((groups, rows - 1) + out_ref.shape[2:], jnp.float32)
+    out_ref[:, rows - 1] = jnp.full((groups,) + out_ref.shape[2:], -1.0, jnp.float32)
+    weights = coarsen_weights(width)
+    lane = lax.broadcasted_iota(jnp.int32, out_ref.shape[2:], 1)
+    for part in range(tiles // chunk):
+        fetch(part).wait()
+        trace = trace_ref[pl.ds(part * chunk, chunk)].reshape(chunk * nfield * levels, width)
+        cells = jnp.dot(
+            trace, weights, precision=HIGHEST, preferred_element_type=jnp.float32
+        ).reshape((chunk, slab) + out_ref.shape[2:])
+        for i in range(chunk):
+            tile = part * chunk + i
+            target = gx_ref[tile]
+            rank = seen_ref[target]
+            seen_ref[target] = rank + 1
+            slot_ref[tile] = target * CAP + rank
+            out_ref[target, pl.ds(rank * slab, slab)] = cells[i]
+            column = jnp.full(lane.shape, col_ref[tile], jnp.int32).astype(jnp.float32)
+            out_ref[target, rows - 1] = jnp.where(lane == rank, column, out_ref[target, rows - 1])
+
+
+def pack_traces(partner_gx, partner_col, fine_fields, groups):
     tiles, nfield, levels, _, width = fine_fields.shape
-    sent = jax.ShapeDtypeStruct((groups * CAP, nfield, levels, width // 2), jnp.float32)
+    slab = nfield * levels // 2
+    sent = jax.ShapeDtypeStruct((groups, CAP * slab + 1, 2, width // 2), jnp.float32)
     return pl.pallas_call(
         pack_kernel,
         out_shape=(sent, jax.ShapeDtypeStruct((tiles,), jnp.int32)),
-        in_specs=[SCALARS, WHOLE],
+        in_specs=[SCALARS, SCALARS, pl.BlockSpec(memory_space=pl.ANY)],
         out_specs=(WHOLE, SCALARS),
-        scratch_shapes=[pltpu.SMEM((groups,), jnp.int32)],
+        scratch_shapes=[
+            pltpu.VMEM((tiles, nfield, levels, width), jnp.float32),
+            pltpu.SMEM((groups,), jnp.int32),
+            pltpu.SemaphoreType.DMA((4,)),
+        ],
         cost_estimate=cost(10**8, fine_fields, sent),
+        name="pack_traces",
+    )(partner_gx, partner_col, fine_fields)
+
+
+def answer_kernel(came_ref, q_ref, out_ref):
+    nfield, levels, columns, _ = q_ref.shape
+    groups, rows = came_ref.shape[:2]
+    asked = came_ref[:, rows - 1, 0, :]
+    column = lax.broadcasted_iota(jnp.int32, (groups, columns), 1).astype(jnp.float32)
+    for rank in range(CAP):
+        picked = jnp.where(asked[:, rank : rank + 1] == column, 1.0, 0.0)
+        for row in range(nfield * levels):
+            trace = jnp.dot(
+                picked,
+                q_ref[row // levels, row % levels],
+                precision=HIGHEST,
+                preferred_element_type=jnp.float32,
+            )
+            at = rank * nfield * levels + row
+            out_ref[:, at // 2, at % 2, :] = trace
+
+
+def answer_requests(came, fields):
+    nfield, levels, _, span = fields.shape
+    shape = (came.shape[0], CAP * nfield * levels // 2, 2, span)
+    return pl.pallas_call(
+        answer_kernel,
+        out_shape=jax.ShapeDtypeStruct(shape, jnp.float32),
+        in_specs=[WHOLE, WHOLE],
+        out_specs=WHOLE,
         compiler_params=pltpu.CompilerParams(vmem_limit_bytes=VMEM_BYTES),
-        name="pack_traces",
-    )(partner_gx, fine_fields)
+        cost_estimate=cost(10**8, came, fields),
+        name="answer_requests",
+    )(came, fields)
 
 
 def finish_kernel(slot_ref, back_ref, part_ref, out_ref, stage_ref, sems):
@@ -90,8 +145,11 @@
     total = stage_ref.shape[0]
 
     def fetch(tile):
+        slot = slot_ref[tile]
         return pltpu.make_async_copy(
-            back_ref.at[slot_ref[tile]], stage_ref.at[tile], sems.at[tile]
+            back_ref.at[slot // CAP, pl.ds(slot % CAP * stage_ref.shape[1], stage_ref.shape[1])],
+            stage_ref.at[tile],
+            sems.at[tile],
         )
 
     @pl.when(step == 0)
@@ -119,7 +177,7 @@
         in_specs=[SCALARS, pl.BlockSpec(memory_space=pl.ANY), spec],
         out_specs=spec,
         scratch_shapes=[
-            pltpu.VMEM((tiles, nfield, levels, width // 2), jnp.float32),
+            pltpu.VMEM((tiles, nfield * levels // 2, 2, width // 2), jnp.float32),
             pltpu.SemaphoreType.DMA((tiles,)),
         ],
         cost_estimate=cost(10**8, part, part, back),
@@ -200,16 +258,19 @@
     lane = lax.broadcasted_iota(jnp.int32, (columns, span), 1)
     sat_ref[...] = jnp.zeros_like(sat_ref)
 
+    slab = sat_ref.shape[1]
+
     def add_slot(slot, carry):
         column = wanted_ref[slot]
+        rows = pl.ds(slot % CAP * slab, slab)
 
         @pl.when(column >= 0)
         def _():
-            sat_ref[column] += came_ref[slot] - sent_ref[slot]
+            sat_ref[column] += came_ref[slot // CAP, rows] - sent_ref[slot // CAP, rows]
 
         return carry
 
-    lax.fori_loop(0, came_ref.shape[0], add_slot, 0)
+    lax.fori_loop(0, came_ref.shape[0] * CAP, add_slot, 0)
 
     def around(q, which, level):
         row = which * levels + level
@@ -241,7 +302,7 @@
             )
             advect = 0.5 * (u_flow * (east - west) + v_flow * (north - south))
             rate = diffuse - advect + vertical_mix * (above - 2.0 * q + below)
-            sat = coarse_penalty * sat_ref[:, field, level, :]
+            sat = coarse_penalty * sat_ref[:, (field * levels + level) // 2, level % 2, :]
             out_ref[field, level] = q + time_step * (rate + sat)
 
 
@@ -252,7 +313,7 @@
         out_shape=jax.ShapeDtypeStruct(fields.shape, jnp.float32),
         in_specs=[SCALARS] + [WHOLE] * 8,
         out_specs=WHOLE,
-        scratch_shapes=[pltpu.VMEM((columns, nfield, levels, span), jnp.float32)],
+        scratch_shapes=[pltpu.VMEM((columns, nfield * levels // 2, 2, span), jnp.float32)],
         cost_estimate=cost(10**8, fields, fields, came),
         compiler_params=pltpu.CompilerParams(vmem_limit_bytes=VMEM_BYTES),
         name="coarse_step",
@@ -263,76 +324,48 @@
     fields, viscosity, precursor, tile_index, fine_fields, fine_viscosity, partner_gx, partner_col
 ):
     nfield, levels, columns, span_cells = fields.shape
-    tiles = partner_gx.shape[0]
     groups = lax.axis_size("gx")
     my_gx = lax.axis_index("gx")
     my_gy = lax.axis_index("gy")
-    block = (groups, CAP, nfield, levels, span_cells)
-
-    sending, slots = pack_traces(partner_gx, fine_fields, groups)
-    trace_in = lax.all_to_all(sending.reshape(block), "gx", split_axis=0, concat_axis=0, tiled=True)
+    halo = (nfield + 1) * levels
+
+    sending, slots = pack_traces(partner_gx, partner_col, fine_fields, groups)
+    came = lax.all_to_all(sending, "gx", split_axis=0, concat_axis=0, tiled=True)
+    sent = answer_requests(came, fields)
+    returned = lax.all_to_all(sent, "gx", split_axis=0, concat_axis=0, tiled=True)
+    wanted = came[:, -1, 0, :CAP].reshape(groups * CAP).astype(jnp.int32)
 
     rows = jnp.concatenate([fields, viscosity[None]], axis=0)
-    halo = (nfield + 1) * levels
-    request = jnp.concatenate([partner_gx, partner_col]).astype(jnp.float32)[None, :]
-    request = jnp.pad(request, ((0, 0), (0, span_cells - 2 * tiles)))
     low_row = rows[:, :, 0, :].reshape(halo, span_cells)
     high_row = rows[:, :, -1, :].reshape(halo, span_cells)
-    from_west = ring_shift(jnp.concatenate([high_row, request], axis=0), "gx", 1)
+    from_west = ring_shift(high_row, "gx", 1)
     from_east = ring_shift(low_row, "gx", -1)
-    asked = jnp.concatenate([request, from_west[halo:]], axis=0)
-    while asked.shape[0] < groups:
-        asked = jnp.concatenate([asked, ring_shift(asked, "gx", asked.shape[0])], axis=0)
-    order = (
-        jnp.arange(groups)[None, :] == (my_gx - jnp.arange(groups)[:, None]) % groups
-    ).astype(jnp.float32)
-    asked = jnp.einsum("sj,jc->sc", order, asked[:, : 2 * tiles], precision=HIGHEST)
-    mine = asked[:, :tiles] == my_gx.astype(jnp.float32)
-    earlier = jnp.arange(tiles)[None, :] < jnp.arange(tiles)[:, None]
-    before = jnp.sum(jnp.where(earlier, mine[:, None, :], False).astype(jnp.int32), axis=2)
-    wanted = []
-    for rank in range(CAP):
-        chosen = mine & (before == rank)
-        wanted.append(jnp.sum(jnp.where(chosen, asked[:, tiles:] + 1.0, 0.0), axis=1) - 1.0)
-    wanted = jnp.stack(wanted, axis=1)
-    column_in = (wanted[:, :, None] == jnp.arange(columns, dtype=jnp.float32)).astype(jnp.float32)
-    answer = jnp.einsum("gsx,fzxy->gsfzy", column_in, fields, precision=HIGHEST)
-    returned = lax.all_to_all(answer, "gx", split_axis=0, concat_axis=0, tiled=True)
-
     low_col = rows[:, :, :, 0].reshape(halo, columns)
     high_col = rows[:, :, :, -1].reshape(halo, columns)
     width = precursor.shape[2]
     shard = precursor.reshape(nfield * levels, width)
     from_south = ring_shift(jnp.concatenate([high_col, shard], axis=0), "gy", 1)
     from_north = ring_shift(low_col, "gy", -1)
-    shards = jnp.stack([shard, from_south[halo:]])
     count = lax.axis_size("gy")
-    while shards.shape[0] < count:
-        shards = jnp.concatenate([shards, ring_shift(shards, "gy", shards.shape[0])], axis=0)
+    near = [shard, from_south[halo:]] + [ring_shift(shard, "gy", s) for s in (2, 3)]
+    near = jnp.concatenate(near, axis=0)
+    shards = [near] + [ring_shift(near, "gy", s) for s in range(4, count, 4)]
+    shards = jnp.concatenate(shards, axis=0).reshape(-1, nfield * levels, width)
     position = ((my_gy - tile_index // width) % count) * width + tile_index % width
-    choose = (position[:, None] == jnp.arange(count * width)[None, :]).astype(jnp.float32)
+    choose = (position[:, None] == jnp.arange(shards.shape[0] * width)[None, :]).astype(jnp.float32)
     inflow = jnp.einsum(
-        "jro,yjo->ry", shards, choose.reshape(-1, count, width), precision=HIGHEST
+        "jro,yjo->ry", shards, choose.reshape(-1, shards.shape[0], width), precision=HIGHEST
     )
 
     inlet = jnp.concatenate([inflow, viscosity[:, 0, :]], axis=0)
-    west = jnp.where(my_gx == 0, inlet, from_west[:halo])
+    west = jnp.where(my_gx == 0, inlet, from_west)
     east = jnp.where(my_gx == groups - 1, high_row, from_east)
-    slab = (groups * CAP,) + block[2:]
     fields_out = coarse_step(
-        wanted.reshape(groups * CAP).astype(jnp.int32),
-        fields,
-        viscosity,
-        west,
-        east,
-        from_south[:halo].T,
-        from_north.T,
-        trace_in.reshape(slab),
-        answer.reshape(slab),
+        wanted, fields, viscosity, west, east, from_south[:halo].T, from_north.T, came, sent
     )
 
     part = fine_step(fine_fields, fine_viscosity)
-    fine_out = finish_tiles(slots, returned.reshape(slab), part)
+    fine_out = finish_tiles(slots, returned, part)
     return (fields_out, fine_out)
 
 

time: 159 us -> 119 us (0.75)
  the two profiles are of different devices: /device:TPU:16 before, /device:TPU:1 now
where the time goes in v2:
time: 119 us
  blocking collectives  55.3 us (46%)
  starting transfers between devices  37.3 us (31%)
  Pallas kernels  16.1 us (14%)
  waiting for transfers between devices  6.01 us (5%)
  local copies, waits for them, and re-layouts  1.77 us (1%)
    all_to_all x1, blocking collectives, on_device(): lax.all_to_all(sending, 'gx', split_axis=0, concat_axis=0, tiled=True)  55.3 us
    ppermute x9, starting transfers between devices, ring_shift(): lax.ppermute(cells, axis, [(i, (i + step) % count) for i in range(count)])  32 us
    ppermute x9, waiting for transfers between devices, ring_shift(): lax.ppermute(cells, axis, [(i, (i + step) % count) for i in range(count)])  6.01 us
    all_to_all x1, starting transfers between devices, on_device(): lax.all_to_all(sent, 'gx', split_axis=0, concat_axis=0, tiled=True)  5.32 us
    pallas_call x1, Pallas kernels, coarse_step(): pl.pallas_call(coarse_kernel, out_shape=jax.ShapeDtypeStruct(fields.shape...  4.25 us
    pallas_call x1, Pallas kernels, pack_traces(): pl.pallas_call(pack_kernel, out_shape=(sent, jax.ShapeDtypeStruct((tiles,...  3.53 us
    pallas_call x1, Pallas kernels, finish_tiles(): pl.pallas_call(finish_kernel, grid=(tiles // block,), out_shape=jax.Shape...  3.33 us
    pallas_call x1, Pallas kernels, fine_step(): pl.pallas_call(fine_kernel, grid=(tiles // block,), out_shape=jax.ShapeDt...  3.09 us
  transfers between devices with their start and end apart: 10, of which 2 were waited for; matrix products, arithmetic and copies ran while one was open for 2% of the time, Pallas kernels for 6%

profile of v2, /device:TPU:1, one launch (start us, length us, event | category | flops | bytes accessed | tf_op | source)
XLA Modules:
  0.0 118.6 jit_solution(5690725505455913190)
XLA Ops:
  0.6 0.0 copy-start
  0.6 3.5 %pack_traces.1 = (f32[32,21,2,128]{3,2,1,0:T(2,128)}, s32[16]{0:T(128)}) custom-call(s32[16]{0:T(128)} %gx_ref.1, s32[16]{0:T(128)} %col_ref.1, f32[16,5,4,4,256]{4,3,2,1,0:T(4,128)} %q_ref.5), custom_call_target="tpu_custom_call" | custom-call | flops 100000000 | bytes 1998848 | tf_op jit(solution)/shard_map/pack_traces/pallas_call | solution.py:95
  4.2 55.3 %all_to_all.10.came_ref = f32[32,21,2,128]{3,2,1,0:T(2,128)S(1)} all-to-all(f32[32,21,2,128]{3,2,1,0:T(2,128)} %get-tuple-element.4), channel_id=1, replica_groups=mesh['gx'=32,'gy'=16] {'gx'}, dimensions={0} | all-to-all | bytes 1376256 | tf_op jit(solution)/shard_map/all_to_all | solution.py:333
  59.4 0.0 copy-done
  59.4 1.9 %answer_requests.1.sent_ref = f32[32,20,2,128]{3,2,1,0:T(2,128)} custom-call(f32[32,21,2,128]{3,2,1,0:T(2,128)S(1)} %all_to_all.10.came_ref, f32[5,4,32,128]{3,2,1,0:T(8,128)S(1)} %copy-done), custom_call_target="tpu_custom_call" | custom-call | flops 100000000 | bytes 1015808 | tf_op jit(solution)/shard_map/answer_requests/pallas_call | solution.py:131
  61.4 5.3 %all-to-all-start.1 = ((f32[32,20,2,128]{3,2,1,0:T(2,128)}), f32[32,20,2,128]{3,2,1,0:T(2,128)S(1)}, u32[]{:S(2)}, u32[]{:S(2)}) async-start(f32[32,20,2,128]{3,2,1,0:T(2,128)} %answer_requests.1.sent_ref), calls=%async_computation.1 | async-start | bytes 1310720 | tf_op jit(solution)/shard_map/all_to_all | solution.py:335
  66.7 0.0 copy-done.7
  66.7 0.1 copy.20
  66.8 5.6 %collective-permute-start.2 = (f32[20,32]{0,1:T(8,128)S(1)}, f32[20,32]{0,1:T(8,128)S(1)}, u32[]{:S(2)}, u32[]{:S(2)}) collective-permute-start(f32[20,32]{0,1:T(8,128)S(1)} %copy.20), channel_id=1, source_target_pairs={{0,3},{1,4},{2,5},{3,6},{4,7},{5,8},{6,9},{7,10},{8,11},{9,12},{10... | collective-permute-start | bytes 7688 | tf_op jit(solution)/shard_map/ppermute | solution.py:47
  72.4 2.2 %collective-permute-start.1 = (f32[20,32]{0,1:T(8,128)S(1)}, f32[20,32]{0,1:T(8,128)S(1)}, u32[]{:S(2)}, u32[]{:S(2)}) collective-permute-start(f32[20,32]{0,1:T(8,128)S(1)} %copy.20), channel_id=1, source_target_pairs={{0,2},{1,3},{2,4},{3,5},{4,6},{5,7},{6,8},{7,9},{8,10},{9,11},{10,... | collective-permute-start | bytes 7688 | tf_op jit(solution)/shard_map/ppermute | solution.py:47
  74.6 0.0 copy-done.4
  74.7 5.6 %collective-permute-start.7 = (f32[24,128]{1,0:T(8,128)S(1)}, f32[24,128]{1,0:T(8,128)S(1)}, u32[]{:S(2)}, u32[]{:S(2)}) collective-permute-start(f32[24,128]{1,0:T(8,128)S(1)} %bitcast.23), channel_id=1, source_target_pairs={{0,496},{16,0},{32,16},{48,32},{64,48},{80,64},{96,80},{112,96},{1... | collective-permute-start | bytes 36872 | tf_op jit(solution)/shard_map/ppermute | solution.py:47
  80.3 1.9 %collective-permute-start.6 = (f32[24,128]{1,0:T(8,128)S(1)}, f32[24,128]{1,0:T(8,128)S(1)}, u32[]{:S(2)}, u32[]{:S(2)}) collective-permute-start(f32[24,128]{1,0:T(8,128)S(1)} %bitcast.21), channel_id=1, source_target_pairs={{0,16},{16,32},{32,48},{48,64},{64,80},{80,96},{96,112},{112,128},... | collective-permute-start | bytes 36872 | tf_op jit(solution)/shard_map/ppermute | solution.py:47
  82.2 0.4 fusion.2
  82.6 0.1 copy.15
  82.7 0.1 pad_maximum_fusion.1
  82.8 1.9 %collective-permute-start = (f32[44,32]{0,1:T(8,128)S(1)}, f32[44,32]{0,1:T(8,128)S(1)}, u32[]{:S(2)}, u32[]{:S(2)}) collective-permute-start(f32[44,32]{0,1:T(8,128)S(1)} %pad_maximum_fusion.1), channel_id=1, source_target_pairs={{0,1},{1,2},{2,3},{3,4},{4,5},{5,6},{6,7},{7,8},{8,9},{9,10},{10,1... | collective-permute-start | bytes 16904 | tf_op jit(solution)/shard_map/ppermute | solution.py:47
  84.7 0.0 copy-done.8
  84.8 0.1 broadcast_compare_fusion
  84.9 3.1 %fine_step.1.part_ref = f32[16,5,4,4,256]{4,3,2,1,0:T(4,128)S(1)} custom-call(f32[16,5,4,4,256]{4,3,2,1,0:T(4,128)S(1)} %copy-done.1, f32[16,4,4,256]{3,2,1,0:T(4,128)S(1)} %copy-done.5), custom_call_target="tpu_custom_call" | custom-call | flops 100000000 | bytes 2883584 | tf_op jit(solution)/shard_map/fine_step/pallas_call | solution.py:232
  88.0 0.0 copy-start.2
  88.0 1.0 copy-done.2
  89.1 0.1 copy.23
  89.2 0.0 collective-permute-done
  89.2 4.6 %collective-permute-start.8 = (f32[24,32]{0,1:T(8,128)S(1)}, f32[24,32]{0,1:T(8,128)S(1)}, u32[]{:S(2)}, u32[]{:S(2)}) collective-permute-start(f32[24,32]{0,1:T(8,128)S(1)} %copy.23), channel_id=1, source_target_pairs={{0,15},{1,0},{2,1},{3,2},{4,3},{5,4},{6,5},{7,6},{8,7},{9,8},{10,9... | collective-permute-start | bytes 9224 | tf_op jit(solution)/shard_map/ppermute | solution.py:47
  93.8 0.1 slice.35
  93.9 0.0 collective-permute-done.2
  93.9 0.0 collective-permute-done.1
  93.9 0.1 pad_maximum_fusion.2
  93.9 4.4 %collective-permute-start.5 = (f32[80,32]{0,1:T(8,128)S(1)}, f32[80,32]{0,1:T(8,128)S(1)}, u32[]{:S(2)}, u32[]{:S(2)}) collective-permute-start(f32[80,32]{0,1:T(8,128)S(1)} %pad_maximum_fusion.2), channel_id=1, source_target_pairs={{0,12},{1,13},{2,14},{3,15},{4,0},{5,1},{6,2},{7,3},{8,4},{9,5},{1... | collective-permute-start | bytes 30728 | tf_op jit(solution)/shard_map/ppermute | solution.py:47
  98.4 3.3 %collective-permute-start.4 = (f32[80,32]{0,1:T(8,128)S(1)}, f32[80,32]{0,1:T(8,128)S(1)}, u32[]{:S(2)}, u32[]{:S(2)}) collective-permute-start(f32[80,32]{0,1:T(8,128)S(1)} %pad_maximum_fusion.2), channel_id=1, source_target_pairs={{0,8},{1,9},{2,10},{3,11},{4,12},{5,13},{6,14},{7,15},{8,0},{9,1},... | collective-permute-start | bytes 30728 | tf_op jit(solution)/shard_map/ppermute | solution.py:47
  101.7 0.0 collective-permute-done.7
  101.7 2.4 %collective-permute-start.3 = (f32[80,32]{0,1:T(8,128)S(1)}, f32[80,32]{0,1:T(8,128)S(1)}, u32[]{:S(2)}, u32[]{:S(2)}) collective-permute-start(f32[80,32]{0,1:T(8,128)S(1)} %pad_maximum_fusion.2), channel_id=1, source_target_pairs={{0,4},{1,5},{2,6},{3,7},{4,8},{5,9},{6,10},{7,11},{8,12},{9,13},{1... | collective-permute-start | bytes 30728 | tf_op jit(solution)/shard_map/ppermute | solution.py:47
  104.1 0.0 collective-permute-done.5
  104.1 0.5 collective-permute-done.4
  104.7 5.5 %collective-permute-done.3 = f32[80,32]{0,1:T(8,128)S(1)} collective-permute-done((f32[80,32]{0,1:T(8,128)S(1)}, f32[80,32]{0,1:T(8,128)S(1)}, u32[]{:S(2)}, u32[]{:S(2)}) %collective-permute-start.3) | collective-permute-done | bytes 10272 | tf_op jit(solution)/shard_map/ppermute | solution.py:47
  110.1 0.1 concatenate.19
  110.2 0.2 reshape.31
  110.4 0.0 copy-start.3
  110.4 0.4 convolution_bitcast_fusion
  110.8 0.0 collective-permute-done.6
  110.8 0.1 fusion.4
  110.9 0.1 convert_element_type.7.wanted_ref
  111.0 0.0 collective-permute-done.8
  111.0 4.2 %coarse_step.1 = f32[5,4,32,128]{3,2,1,0:T(8,128)} custom-call(s32[64]{0:T(128)S(1)} %convert_element_type.7.wanted_ref, f32[5,4,32,128]{3,2,1,0:T(8,128)S(1)} %copy-done, f32[4,32,128]{2,1,0:T(8,128)S(1)} %copy-done.4, f32[24,128]{1,0:T(8,128)S(1)} %maximum_select_fusion.west_ref, f32[24,128]{1,0:T(8,128)S(1)} %broadcast_select_fusion.east_ref, ...), custom_call_target="tpu_custom_call" | custom-call | flops 100000000 | bytes 1343488 | tf_op jit(solution)/shard_map/coarse_step/pallas_call | solution.py:311
  115.2 0.0 all-to-all-done.1.back_ref
  115.2 0.0 copy-done.3
  115.2 3.3 %finish_tiles.1 = f32[16,5,4,4,256]{4,3,2,1,0:T(4,128)} custom-call(s32[16]{0:T(128)S(1)} %copy-done.6, f32[32,20,2,128]{3,2,1,0:T(2,128)S(1)} %all-to-all-done.1.back_ref, f32[16,5,4,4,256]{4,3,2,1,0:T(4,128)S(1)} %copy-done.3), custom_call_target="tpu_custom_call" | custom-call | flops 100000000 | bytes 3276800 | tf_op jit(solution)/shard_map/finish_tiles/pallas_call | solution.py:173
  (17 shorter events, 0.1 us)
Async XLA Ops:
  0.6 58.8 %copy-start = (f32[5,4,32,128]{3,2,1,0:T(8,128)S(1)}, f32[5,4,32,128]{3,2,1,0:T(8,128)}, u32[]{:S(2)}) copy-start(f32[5,4,32,128]{3,2,1,0:T(8,128)} %q_ref.4) | copy-start | bytes 983044
  59.4 7.3 %copy-start.7 = (f32[5,4,32]{2,1,0:T(4,128)S(1)}, f32[5,4,32]{2,1,0:T(4,128)}, u32[]{:S(2)}) copy-start(f32[5,4,32]{2,1,0:T(4,128)} %param.10) | copy-start | bytes 7684
  59.4 15.2 %copy-start.4 = (f32[4,32,128]{2,1,0:T(8,128)S(1)}, f32[4,32,128]{2,1,0:T(8,128)}, u32[]{:S(2)}) copy-start(f32[4,32,128]{2,1,0:T(8,128)} %nu_ref.2) | copy-start | bytes 196612
  61.3 23.4 %copy-start.8 = (s32[128]{0:T(128)S(1)}, s32[128]{0:T(128)}, u32[]{:S(2)}) copy-start(s32[128]{0:T(128)} %param.11) | copy-start | bytes 1540
  61.4 23.6 %copy-start.1 = (f32[16,5,4,4,256]{4,3,2,1,0:T(4,128)S(1)}, f32[16,5,4,4,256]{4,3,2,1,0:T(4,128)}, u32[]{:S(2)}) copy-start(f32[16,5,4,4,256]{4,3,2,1,0:T(4,128)} %q_ref.5) | copy-start | bytes 3932164
  61.4 23.6 %copy-start.5 = (f32[16,4,4,256]{3,2,1,0:T(4,128)S(1)}, f32[16,4,4,256]{3,2,1,0:T(4,128)}, u32[]{:S(2)}) copy-start(f32[16,4,4,256]{3,2,1,0:T(4,128)} %nu_ref.3) | copy-start | bytes 786436
  61.4 53.9 %all-to-all-start.1 = ((f32[32,20,2,128]{3,2,1,0:T(2,128)}), f32[32,20,2,128]{3,2,1,0:T(2,128)S(1)}, u32[]{:S(2)}, u32[]{:S(2)}) async-start(f32[32,20,2,128]{3,2,1,0:T(2,128)} %answer_requests.1.sent_ref), calls=%async_computation.1 | async-start | bytes 1310720 | tf_op jit(solution)/shard_map/all_to_all | solution.py:335
  66.8 27.1 %collective-permute-start.2 = (f32[20,32]{0,1:T(8,128)S(1)}, f32[20,32]{0,1:T(8,128)S(1)}, u32[]{:S(2)}, u32[]{:S(2)}) collective-permute-start(f32[20,32]{0,1:T(8,128)S(1)} %copy.20), channel_id=1, source_target_pairs={{0,3},{1,4},{2,5},{3,6},{4,7},{5,8},{6,9},{7,10},{8,11},{9,12},{10... | collective-permute-start | bytes 7688 | tf_op jit(solution)/shard_map/ppermute | solution.py:47
  72.4 21.5 %collective-permute-start.1 = (f32[20,32]{0,1:T(8,128)S(1)}, f32[20,32]{0,1:T(8,128)S(1)}, u32[]{:S(2)}, u32[]{:S(2)}) collective-permute-start(f32[20,32]{0,1:T(8,128)S(1)} %copy.20), channel_id=1, source_target_pairs={{0,2},{1,3},{2,4},{3,5},{4,6},{5,7},{6,8},{7,9},{8,10},{9,11},{10,... | collective-permute-start | bytes 7688 | tf_op jit(solution)/shard_map/ppermute | solution.py:47
  74.7 27.1 %collective-permute-start.7 = (f32[24,128]{1,0:T(8,128)S(1)}, f32[24,128]{1,0:T(8,128)S(1)}, u32[]{:S(2)}, u32[]{:S(2)}) collective-permute-start(f32[24,128]{1,0:T(8,128)S(1)} %bitcast.23), channel_id=1, source_target_pairs={{0,496},{16,0},{32,16},{48,32},{64,48},{80,64},{96,80},{112,96},{1... | collective-permute-start | bytes 36872 | tf_op jit(solution)/shard_map/ppermute | solution.py:47
  80.3 30.5 %collective-permute-start.6 = (f32[24,128]{1,0:T(8,128)S(1)}, f32[24,128]{1,0:T(8,128)S(1)}, u32[]{:S(2)}, u32[]{:S(2)}) collective-permute-start(f32[24,128]{1,0:T(8,128)S(1)} %bitcast.21), channel_id=1, source_target_pairs={{0,16},{16,32},{32,48},{48,64},{64,80},{80,96},{96,112},{112,128},... | collective-permute-start | bytes 36872 | tf_op jit(solution)/shard_map/ppermute | solution.py:47
  82.8 6.4 %collective-permute-start = (f32[44,32]{0,1:T(8,128)S(1)}, f32[44,32]{0,1:T(8,128)S(1)}, u32[]{:S(2)}, u32[]{:S(2)}) collective-permute-start(f32[44,32]{0,1:T(8,128)S(1)} %pad_maximum_fusion.1), channel_id=1, source_target_pairs={{0,1},{1,2},{2,3},{3,4},{4,5},{5,6},{6,7},{7,8},{8,9},{9,10},{10,1... | collective-permute-start | bytes 16904 | tf_op jit(solution)/shard_map/ppermute | solution.py:47
  88.0 1.1 copy-start.2
  89.2 21.8 %collective-permute-start.8 = (f32[24,32]{0,1:T(8,128)S(1)}, f32[24,32]{0,1:T(8,128)S(1)}, u32[]{:S(2)}, u32[]{:S(2)}) collective-permute-start(f32[24,32]{0,1:T(8,128)S(1)} %copy.23), channel_id=1, source_target_pairs={{0,15},{1,0},{2,1},{3,2},{4,3},{5,4},{6,5},{7,6},{8,7},{9,8},{10,9... | collective-permute-start | bytes 9224 | tf_op jit(solution)/shard_map/ppermute | solution.py:47
  93.9 10.2 %collective-permute-start.5 = (f32[80,32]{0,1:T(8,128)S(1)}, f32[80,32]{0,1:T(8,128)S(1)}, u32[]{:S(2)}, u32[]{:S(2)}) collective-permute-start(f32[80,32]{0,1:T(8,128)S(1)} %pad_maximum_fusion.2), channel_id=1, source_target_pairs={{0,12},{1,13},{2,14},{3,15},{4,0},{5,1},{6,2},{7,3},{8,4},{9,5},{1... | collective-permute-start | bytes 30728 | tf_op jit(solution)/shard_map/ppermute | solution.py:47
  98.4 6.3 %collective-permute-start.4 = (f32[80,32]{0,1:T(8,128)S(1)}, f32[80,32]{0,1:T(8,128)S(1)}, u32[]{:S(2)}, u32[]{:S(2)}) collective-permute-start(f32[80,32]{0,1:T(8,128)S(1)} %pad_maximum_fusion.2), channel_id=1, source_target_pairs={{0,8},{1,9},{2,10},{3,11},{4,12},{5,13},{6,14},{7,15},{8,0},{9,1},... | collective-permute-start | bytes 30728 | tf_op jit(solution)/shard_map/ppermute | solution.py:47
  101.7 8.4 %collective-permute-start.3 = (f32[80,32]{0,1:T(8,128)S(1)}, f32[80,32]{0,1:T(8,128)S(1)}, u32[]{:S(2)}, u32[]{:S(2)}) collective-permute-start(f32[80,32]{0,1:T(8,128)S(1)} %pad_maximum_fusion.2), channel_id=1, source_target_pairs={{0,4},{1,5},{2,6},{3,7},{4,8},{5,9},{6,10},{7,11},{8,12},{9,13},{1... | collective-permute-start | bytes 30728 | tf_op jit(solution)/shard_map/ppermute | solution.py:47
  110.4 4.8 %copy-start.3 = (f32[16,5,4,4,256]{4,3,2,1,0:T(4,128)S(1)}, f32[16,5,4,4,256]{4,3,2,1,0:T(4,128)}, u32[]{:S(2)}) copy-start(f32[16,5,4,4,256]{4,3,2,1,0:T(4,128)} %copy-done.2) | copy-start | bytes 3932164
  110.4 4.8 %copy-start.6 = (s32[16]{0:T(128)S(1)}, s32[16]{0:T(128)}, u32[]{:S(2)}) copy-start(s32[16]{0:T(128)} %get-tuple-element.5.slot_ref) | copy-start | bytes 196
